TPU v7x, 256 devices: a whole 4x4x8 slice. The times are simulated.
256 devices in a mesh: dp: 8 (over y, core), ctx: 32 (over x, z).
Axes of the slice: x: 4, y: 4, z: 8, core: 2. Of those that a mesh axis runs over, the one named last changes fastest.
Arguments:
- query_act: bfloat16 [32768, 4096], P(('dp', 'ctx')), may hold values from -6 to 6
- key_act: bfloat16 [32768, 4096], P(('dp', 'ctx')), may hold values from -6 to 6
- value_act: bfloat16 [32768, 4096], P(('dp', 'ctx')), may hold values from -6 to 6
- out_grad: bfloat16 [32768, 4096], P(('dp', 'ctx')), may hold values from -6 to 6
- filter_taps: float32 [4096, 128], P('ctx'), may hold values from -0.5 to 0.5
- doc_ids: int32 [32768], replicated, may hold values from 0 to 7, as said below
Outputs:
- query_grad: bfloat16 [32768, 4096], P(('dp', 'ctx'))
- key_grad: bfloat16 [32768, 4096], P(('dp', 'ctx'))
- value_grad: bfloat16 [32768, 4096], P(('dp', 'ctx'))
- filter_grad: float32 [4096, 128], P('ctx')
Inputs may be any that keep to these rules, and one draw needn't show every extreme that they name: `doc_ids`: the document numbers start at 0, never fall, and rise by one at each boundary; the window holds 8 documents, each of at least 256 positions.
All inputs are finite; a program needn't handle non-finite values.
Results may differ from a plain program's by a relative error of at most 0.0064.
Values may be sent and summed in bfloat16 or wider, within the bound.
A program may use at most 192 MiB of HBM per device.

v0:
```python
import math

import jax
import jax.numpy as jnp
from jax import lax
from jax.sharding import PartitionSpec as P


def from_behind(value, axis, steps):
    count = lax.axis_size(axis)
    leading, last = (max(0, -steps), min(count, count - steps))
    return lax.ppermute(value, axis, [(source, source + steps) for source in range(leading, last)])


def build_toeplitz(tap_rows):
    chan_count, tap_count = tap_rows.shape
    zero_col = jnp.zeros((chan_count, 1), tap_rows.dtype)
    tail_cols = jnp.zeros((chan_count, tap_count), tap_rows.dtype)
    pattern = jnp.concatenate([zero_col, tap_rows[:, ::-1], tail_cols], axis=1)
    tiled = jnp.tile(pattern, (1, tap_count))[:, : tap_count * 2 * tap_count]
    return tiled.reshape(chan_count, tap_count, 2 * tap_count)


def lag_sums(block):
    chan_count, tap_count, span = block.shape
    flat = block.reshape(chan_count, tap_count * span)
    flat = jnp.pad(flat, ((0, 0), (0, tap_count)))
    skewed = flat.reshape(chan_count, tap_count, span + 1)
    summed = jnp.sum(skewed[:, :, 1 : tap_count + 1], axis=1)
    return summed[:, ::-1]


def mix_block(kv_ext, g_ext, seg_ext, tap_rows):
    chan_count, tap_count = tap_rows.shape
    block_count = kv_ext.shape[1] // tap_count - 1
    kv_blocks = kv_ext.reshape(chan_count, block_count + 1, tap_count)
    windows = jnp.concatenate([kv_blocks[:, :-1], kv_blocks[:, 1:]], axis=2)
    seg_blocks = seg_ext.reshape(block_count + 2, tap_count)
    seg_win = jnp.concatenate([seg_blocks[:-1], seg_blocks[1:]], axis=1)
    same = (seg_win == seg_win[:, -1:]).astype(jnp.bfloat16)
    other = (seg_win != seg_win[:, -1:]).astype(jnp.bfloat16)
    rows_same = same[:, tap_count:]
    rows_other = other[:, tap_count:]
    toeplitz = build_toeplitz(tap_rows)
    kv_same = same[:block_count] * windows
    kv_other = other[:block_count] * windows
    z_same = jnp.einsum("cij,cbj->cbi", toeplitz, kv_same, preferred_element_type=jnp.float32)
    z_other = jnp.einsum("cij,cbj->cbi", toeplitz, kv_other, preferred_element_type=jnp.float32)
    mixed = rows_same[:block_count] * z_same + rows_other[:block_count] * z_other
    g_blocks = g_ext.reshape(chan_count, block_count + 1, tap_count)
    g_same = rows_same * g_blocks
    g_other = rows_other * g_blocks
    d_same = jnp.einsum("cij,cbi->cbj", toeplitz, g_same, preferred_element_type=jnp.float32)
    d_other = jnp.einsum("cij,cbi->cbj", toeplitz, g_other, preferred_element_type=jnp.float32)
    d_win = same * d_same + other * d_other
    back = d_win[:, :block_count, tap_count:] + d_win[:, 1:, :tap_count]
    outer = jnp.einsum(
        "cbi,cbj->cij", g_same[:, :block_count], kv_same, preferred_element_type=jnp.float32
    )
    outer = outer + jnp.einsum(
        "cbi,cbj->cij", g_other[:, :block_count], kv_other, preferred_element_type=jnp.float32
    )
    row_count = block_count * tap_count
    return (
        mixed.reshape(chan_count, row_count),
        back.reshape(chan_count, row_count),
        lag_sums(outer),
    )


def shards(query_act, key_act, value_act, out_grad, filter_taps, doc_ids):
    tap_count = filter_taps.shape[1]
    product = (key_act.astype(jnp.float32) * value_act.astype(jnp.float32)).astype(jnp.bfloat16)
    gated = (query_act.astype(jnp.float32) * out_grad.astype(jnp.float32)).astype(jnp.bfloat16)
    taps_local = filter_taps.astype(jnp.bfloat16)
    scale = 1.0 / math.sqrt(doc_ids.shape[0])
    seg_pad = jnp.pad(doc_ids, (tap_count, tap_count))
    kv_chan, g_chan = (
        lax.all_to_all(product, "ctx", split_axis=1, concat_axis=0, tiled=True),
        lax.all_to_all(gated, "ctx", split_axis=1, concat_axis=0, tiled=True),
    )
    group_rows = kv_chan.shape[0]
    kv_major = kv_chan.T
    g_major = g_chan.T
    prior = from_behind(kv_major[:, group_rows - tap_count :], "dp", 1)
    after = from_behind(g_major[:, :tap_count], "dp", -1)
    kv_ext = jnp.concatenate([prior, kv_major], 1)
    g_ext = jnp.concatenate([g_major, after], 1)
    start = lax.axis_index("dp") * group_rows
    seg_ext = lax.dynamic_slice_in_dim(seg_pad, start, group_rows + 2 * tap_count)
    mixed, back, partial_value = mix_block(kv_ext, g_ext, seg_ext, taps_local)
    mixed_tok, back_tok = (
        lax.all_to_all(
            mixed.T.astype(jnp.bfloat16), "ctx", split_axis=0, concat_axis=1, tiled=True
        ),
        lax.all_to_all(back.T.astype(jnp.bfloat16), "ctx", split_axis=0, concat_axis=1, tiled=True),
    )
    filter_total = lax.psum(partial_value, "dp")
    mixed_f = mixed_tok.astype(jnp.float32)
    back_f = back_tok.astype(jnp.float32)
    query_grad = (out_grad.astype(jnp.float32) * mixed_f).astype(jnp.bfloat16)
    key_grad = (back_f * value_act.astype(jnp.float32)).astype(jnp.bfloat16)
    value_grad = (back_f * key_act.astype(jnp.float32)).astype(jnp.bfloat16)
    return (query_grad, key_grad, value_grad, filter_total * scale)


def solution(mesh):
    in_specs = (
        P(("dp", "ctx"), None),
        P(("dp", "ctx"), None),
        P(("dp", "ctx"), None),
        P(("dp", "ctx"), None),
        P("ctx", None),
        P(),
    )
    out_specs = (
        P(("dp", "ctx"), None),
        P(("dp", "ctx"), None),
        P(("dp", "ctx"), None),
        P("ctx", None),
    )
    return jax.shard_map(shards, mesh=mesh, in_specs=in_specs, out_specs=out_specs, check_vma=False)
```

profile of v0, /device:TPU:1, one launch (start us, length us, event | category | flops | bytes accessed | tf_op | source)
XLA Modules:
  0.0 367.8 jit_solution(12144173972774626496)
XLA Ops:
  10.8 11.9 %all-to-all-start.2 = ((bf16[128,32,128]{0,2,1:T(8,128)(2,1)}), bf16[128,32,128]{0,2,1:T(8,128)(2,1)S(1)}, u32[]{:S(2)}, u32[]{:S(2)}) async-start(bf16[128,32,128]{0,2,1:T(8,128)(2,1)} %bitcast.12), calls=%async_computation.2 | async-start | bytes 2097152 | tf_op jit(solution)/shard_map/all_to_all | solution.py:80
  23.3 24.1 %all-to-all-done.2 = bf16[128,32,128]{0,2,1:T(8,128)(2,1)S(1)} async-done(((bf16[128,32,128]{0,2,1:T(8,128)(2,1)}), bf16[128,32,128]{0,2,1:T(8,128)(2,1)S(1)}, u32[]{:S(2)}, u32[]{:S(2)}) %all-to-all-start.2) | async-done | bytes 1048608 | tf_op jit(solution)/shard_map/all_to_all | solution.py:80
  48.0 6.9 %collective-permute-start.1 = (bf16[128,128]{0,1:T(8,128)(2,1)S(1)}, bf16[128,128]{0,1:T(8,128)(2,1)S(1)}, u32[]{:S(2)}, u32[]{:S(2)}) collective-permute-start(bf16[128,128]{0,1:T(8,128)(2,1)S(1)} %slice.113), channel_id=1, source_target_pairs={{32,0},{64,32},{96,64},{128,96},{160,128},{192,160},{224,192},{33,... | collective-permute-start | bytes 98312 | tf_op jit(solution)/shard_map/ppermute | solution.py:12
  55.2 4.4 %tile.4 = bf16[128,128,257]{0,2,1:T(8,128)(2,1)} broadcast(bf16[128,257]{0,1:T(8,128)(2,1)S(1)} %copy.72), dimensions={0,2} | broadcast | bytes 8487168 | tf_op jit(solution)/shard_map/tile | solution.py:20
  59.6 12.9 %tile.10 = bf16[128,32896]{0,1:T(8,128)(2,1)} reshape(bf16[128,128,257]{0,2,1:T(8,128)(2,1)} %tile.4) | data formatting | bytes 16842752 | tf_op jit(solution)/shard_map/tile | solution.py:20
  72.5 7.0 %slice.109 = bf16[128,32768]{0,1:T(8,128)(2,1)} slice(bf16[128,32896]{0,1:T(8,128)(2,1)} %tile.10), slice={[0:128], [0:32768]} | slice | bytes 16777216 | tf_op jit(solution)/shard_map/slice | solution.py:20
  79.6 12.7 %copy.90 = bf16[128,128,256]{2,1,0:T(8,128)(2,1)} copy(bf16[128,128,256]{0,2,1:T(8,128)(2,1)} %bitcast.63) | data formatting | bytes 16777216 | tf_op jit(solution)/shard_map/reshape | solution.py:21
  93.9 5.2 %fusion.17 = f32[128,33,256]{2,1,0:T(8,128)S(1)} fusion(bf16[128,33,128]{2,1,0:T(8,128)(2,1)S(1)} %get-tuple-element.23, bf16[128,128,256]{2,1,0:T(8,128)(2,1)} %copy.90), kind=kOutput, calls=%fused_computation.45 | convolution fusion | flops 276824064 | bytes 13795328 | tf_op jit(solution)/shard_map/cij,cbi->cbj/dot_general | solution.py:53
  103.6 4.8 %all-to-all-start.3 = ((bf16[32,128,128]{1,2,0:T(8,128)(2,1)}), bf16[32,128,128]{1,2,0:T(8,128)(2,1)S(1)}, u32[]{:S(2)}, u32[]{:S(2)}) async-start(bf16[32,128,128]{1,2,0:T(8,128)(2,1)} %copy_bitcast_fusion), calls=%async_computation.3 | async-start | bytes 2097152 | tf_op jit(solution)/shard_map/all_to_all | solution.py:96
  112.3 23.8 %all-to-all-done.3 = bf16[32,128,128]{1,2,0:T(8,128)(2,1)S(1)} async-done(((bf16[32,128,128]{1,2,0:T(8,128)(2,1)}), bf16[32,128,128]{1,2,0:T(8,128)(2,1)S(1)}, u32[]{:S(2)}, u32[]{:S(2)}) %all-to-all-start.3) | async-done | bytes 1048608 | tf_op jit(solution)/shard_map/all_to_all | solution.py:96
  139.2 31.3 %all_to_all.64 = bf16[128,32,128]{0,2,1:T(8,128)(2,1)S(1)} all-to-all(bf16[128,32,128]{0,2,1:T(8,128)(2,1)S(1)} %bitcast.75), channel_id=1, replica_groups=mesh['dp'=8,'ctx'=32] {'ctx'}, dimensions={1} | all-to-all | bytes 2097152 | tf_op jit(solution)/shard_map/all_to_all | solution.py:79
  171.3 7.3 %collective-permute-start = (bf16[128,128]{0,1:T(8,128)(2,1)S(1)}, bf16[128,128]{0,1:T(8,128)(2,1)S(1)}, u32[]{:S(2)}, u32[]{:S(2)}) collective-permute-start(bf16[128,128]{0,1:T(8,128)(2,1)S(1)} %slice.106), channel_id=1, source_target_pairs={{0,32},{32,64},{64,96},{96,128},{128,160},{160,192},{192,224},{1,3... | collective-permute-start | bytes 98312 | tf_op jit(solution)/shard_map/ppermute | solution.py:12
  180.1 3.9 %fusion.6 = (bf16[128,32,256]{0,2,1:T(8,128)(2,1)}, bf16[128,32,256]{0,2,1:T(8,128)(2,1)}) fusion(bf16[128,32,128]{0,2,1:T(8,128)(2,1)S(1)} %get-tuple-element.25, bf16[128,32,128]{0,2,1:T(8,128)(2,1)S(1)} %get-tuple-element.24, bf16[32,256]{1,0:T(8,128)(2,1)S(1)} %slice.111, bf16[32,256]{1,0:T(8,128)(2,1)S(1)} %slice.105), kind=kLoop, calls=%fused_computation.17 | loop fusion | flops 9437184 | bytes 6324224 | tf_op jit(solution)/shard_map/mul | solution.py:46
  187.4 4.5 %copy.74 = bf16[128,32,256]{2,1,0:T(8,128)(2,1)} copy(bf16[128,32,256]{0,2,1:T(8,128)(2,1)} %get-tuple-element.21) | data formatting | bytes 4194304 | tf_op jit(solution)/shard_map/mul | solution.py:45
  191.9 7.0 %fusion.16 = f32[128,32,128]{2,1,0:T(8,128)S(1)} fusion(bf16[128,32,256]{2,1,0:T(8,128)(2,1)} %copy.74, bf16[128,128,256]{2,1,0:T(8,128)(2,1)} %copy.90), kind=kOutput, calls=%fused_computation.44 | convolution fusion | flops 268435456 | bytes 12582912 | tf_op jit(solution)/shard_map/cij,cbj->cbi/dot_general | solution.py:47
  198.9 6.5 %add_convert_fusion = bf16[128,32,128]{2,1,0:T(8,128)(2,1)S(1)} fusion(f32[128,32,128]{2,1,0:T(8,128)S(1)} %fusion.16, bf16[128,32,256]{2,1,0:T(8,128)(2,1)S(1)} %copy.75, bf16[128,128,256]{2,1,0:T(8,128)(2,1)} %copy.90, f32[32,128]{1,0:T(8,128)S(1)} %get-tuple-element.33, f32[32,128]{1,0:T(8,128)S(1)} %get-tuple-element.34), kind=kOutput, calls=%fused_computation.16 | convolution fusion | flops 270532608 | bytes 13664256 | tf_op jit(solution)/shard_map/cij,cbj->cbi/dot_general | solution.py:48
  209.0 4.9 %all-to-all-start.1 = ((bf16[32,128,128]{2,1,0:T(8,128)(2,1)}), bf16[32,128,128]{2,1,0:T(8,128)(2,1)}, u32[]{:S(2)}, u32[]{:S(2)}) async-start(bf16[32,128,128]{2,1,0:T(8,128)(2,1)} %bitcast.72), calls=%async_computation.1 | async-start | bytes 2097152 | tf_op jit(solution)/shard_map/all_to_all | solution.py:93
  214.2 9.9 %fusion.9 = f32[128,128,256]{2,1,0:T(8,128)} fusion(bf16[128,32,256]{2,1,0:T(8,128)(2,1)} %copy.74, bf16[128,33,128]{2,1,0:T(8,128)(2,1)S(1)} %get-tuple-element.23), kind=kOutput, calls=%fused_computation.25 | convolution fusion | flops 268435456 | bytes 19922944 | tf_op jit(solution)/shard_map/cbi,cbj->cij/dot_general | solution.py:57
  224.1 14.0 %convolution_add_fusion = f32[128,128,256]{2,1,0:T(8,128)} fusion(f32[128,128,256]{2,1,0:T(8,128)} %fusion.9, bf16[128,32,256]{2,1,0:T(8,128)(2,1)S(1)} %copy.75, bf16[128,33,128]{2,1,0:T(8,128)(2,1)S(1)} %copy-done.1), kind=kOutput, calls=%fused_computation | convolution fusion | flops 272629760 | bytes 36700160 | tf_op jit(solution)/shard_map/cbi,cbj->cij/dot_general | solution.py:60
  238.2 17.9 %copy.91 = f32[128,128,256]{0,2,1:T(8,128)} copy(f32[128,128,256]{2,1,0:T(8,128)} %convolution_add_fusion) | data formatting | bytes 33554432 | tf_op jit(solution)/shard_map/reshape | solution.py:26
  256.1 13.3 %pad.9 = f32[128,32896]{0,1:T(8,128)} pad(f32[128,32768]{0,1:T(8,128)} %bitcast.62, f32[]{:T(128)} %constant.18.clone.1), padding=0_0x0_128 | pad | bytes 33619972 | tf_op jit(solution)/shard_map/jit(_pad)/pad | solution.py:27
  269.4 17.5 %reshape.140 = f32[128,128,257]{0,2,1:T(8,128)} reshape(f32[128,32896]{0,1:T(8,128)} %pad.9) | data formatting | bytes 33685504 | tf_op jit(solution)/shard_map/reshape | solution.py:28
  286.8 4.5 %slice_reduce_fusion = f32[128,128]{0,1:T(8,128)S(1)} fusion(f32[128,128,257]{0,2,1:T(8,128)} %reshape.140), kind=kLoop, calls=%fused_computation.1 | loop fusion | flops 2080768 | bytes 8454144 | tf_op jit(solution)/shard_map/reduce_sum | solution.py:29
  294.7 61.4 %all-reduce.4.cloned.1.call-done = f32[128,128]{0,1:T(8,128)} async-done(((f32[128,128]{0,1:T(8,128)}), f32[128,128]{0,1:T(8,128)}) %all-reduce.4.cloned.1.call-update) | async-done | bytes 65552 | tf_op jit(solution)/shard_map/psum | solution.py:98
  (72 shorter events, 35.7 us)
Async XLA Ops:
  7.2 1.7 copy-start.6
  8.9 2.0 copy-start.2
  9.6 13.2 %copy-start.8 = (f32[128,128]{1,0:T(8,128)S(1)}, f32[128,128]{1,0:T(8,128)}, u32[]{:S(2)}) copy-start(f32[128,128]{1,0:T(8,128)} %param.10) | copy-start | bytes 196612
  9.6 13.3 %copy-start.7 = (s32[32768]{0:T(1024)S(1)}, s32[32768]{0:T(1024)}, u32[]{:S(2)}) copy-start(s32[32768]{0:T(1024)} %param.11) | copy-start | bytes 393220
  10.8 36.5 %all-to-all-start.2 = ((bf16[128,32,128]{0,2,1:T(8,128)(2,1)}), bf16[128,32,128]{0,2,1:T(8,128)(2,1)S(1)}, u32[]{:S(2)}, u32[]{:S(2)}) async-start(bf16[128,32,128]{0,2,1:T(8,128)(2,1)} %bitcast.12), calls=%async_computation.2 | async-start | bytes 2097152 | tf_op jit(solution)/shard_map/all_to_all | solution.py:80
  48.0 44.3 %collective-permute-start.1 = (bf16[128,128]{0,1:T(8,128)(2,1)S(1)}, bf16[128,128]{0,1:T(8,128)(2,1)S(1)}, u32[]{:S(2)}, u32[]{:S(2)}) collective-permute-start(bf16[128,128]{0,1:T(8,128)(2,1)S(1)} %slice.113), channel_id=1, source_target_pairs={{32,0},{64,32},{96,64},{128,96},{160,128},{192,160},{224,192},{33,... | collective-permute-start | bytes 98312 | tf_op jit(solution)/shard_map/ppermute | solution.py:12
  93.9 5.2 %copy-start = (bf16[128,33,128]{2,1,0:T(8,128)(2,1)}, bf16[128,33,128]{2,1,0:T(8,128)(2,1)S(1)}, u32[]{:S(2)}) copy-start(bf16[128,33,128]{2,1,0:T(8,128)(2,1)S(1)} %get-tuple-element.22) | copy-start | bytes 3244036
  93.9 5.2 %slice-start = ((s8[8388608]{0:T(1024)(128)(4,1)}), s8[4194304]{0:T(1024)(128)(4,1)S(1)}, s32[]{:S(2)}) async-start(s8[8388608]{0:T(1024)(128)(4,1)} %bitcast.60), calls=%async_computation.5 | async-start | bytes 8388608
  93.9 6.3 %slice-start.1 = ((s8[8388608]{0:T(1024)(128)(4,1)}), s8[4194304]{0:T(1024)(128)(4,1)S(1)}, s32[]{:S(2)}) async-start(s8[8388608]{0:T(1024)(128)(4,1)} %bitcast.60), calls=%async_computation.6 | async-start | bytes 8388608
  103.6 32.5 %all-to-all-start.3 = ((bf16[32,128,128]{1,2,0:T(8,128)(2,1)}), bf16[32,128,128]{1,2,0:T(8,128)(2,1)S(1)}, u32[]{:S(2)}, u32[]{:S(2)}) async-start(bf16[32,128,128]{1,2,0:T(8,128)(2,1)} %copy_bitcast_fusion), calls=%async_computation.3 | async-start | bytes 2097152 | tf_op jit(solution)/shard_map/all_to_all | solution.py:96
  171.3 8.1 %collective-permute-start = (bf16[128,128]{0,1:T(8,128)(2,1)S(1)}, bf16[128,128]{0,1:T(8,128)(2,1)S(1)}, u32[]{:S(2)}, u32[]{:S(2)}) collective-permute-start(bf16[128,128]{0,1:T(8,128)(2,1)S(1)} %slice.106), channel_id=1, source_target_pairs={{0,32},{32,64},{64,96},{96,128},{128,160},{160,192},{192,224},{1,3... | collective-permute-start | bytes 98312 | tf_op jit(solution)/shard_map/ppermute | solution.py:12
  209.0 148.7 %all-to-all-start.1 = ((bf16[32,128,128]{2,1,0:T(8,128)(2,1)}), bf16[32,128,128]{2,1,0:T(8,128)(2,1)}, u32[]{:S(2)}, u32[]{:S(2)}) async-start(bf16[32,128,128]{2,1,0:T(8,128)(2,1)} %bitcast.72), calls=%async_computation.1 | async-start | bytes 2097152 | tf_op jit(solution)/shard_map/all_to_all | solution.py:93
  213.9 142.2 %all-reduce.4.cloned.1.call-start = ((), (), s32[]{:S(2)}) async-start(), calls=%async_computation.4 | async-start | bytes 131072 | tf_op jit(solution)/shard_map/psum | solution.py:98
  214.2 9.9 %copy-start.1 = (bf16[128,33,128]{2,1,0:T(8,128)(2,1)S(1)}, bf16[128,33,128]{2,1,0:T(8,128)(2,1)}, u32[]{:S(2)}) copy-start(bf16[128,33,128]{2,1,0:T(8,128)(2,1)} %copy-done) | copy-start | bytes 3244036
  286.8 5.2 %copy-start.5 = (bf16[128,4096]{0,1:T(8,128)(2,1)S(1)}, bf16[128,4096]{0,1:T(8,128)(2,1)}, u32[]{:S(2)}) copy-start(bf16[128,4096]{0,1:T(8,128)(2,1)} %get-tuple-element.26) | copy-start | bytes 3145732
  291.4 2.0 copy-start.4
  293.4 65.9 %copy-start.3 = (bf16[128,4096]{0,1:T(8,128)(2,1)S(1)}, bf16[128,4096]{0,1:T(8,128)(2,1)}, u32[]{:S(2)}) copy-start(bf16[128,4096]{0,1:T(8,128)(2,1)} %copy-done.2) | copy-start | bytes 3145732
Sparse Core Ops, SparseCore 0:
  292.2 63.9 all-reduce.3
where the time goes:
time: 371 us; the launch traced here: 368 us
  local copies, waits for them, and re-layouts  117 us (32%)
  waiting for transfers between devices  110 us (30%)
  matrix products  44.3 us (12%)
  starting transfers between devices  35.9 us (10%)
  blocking collectives  31.3 us (8%)
  other arithmetic  14.7 us (4%)
  between operations  14.4 us (4%)
    psum x1, waiting for transfers between devices, shards(): filter_total = lax.psum(partial_value, 'dp')  61.4 us
    all_to_all x1, blocking collectives, shards(): lax.all_to_all(product, 'ctx', split_axis=1, concat_axis=0, tiled=True)  31.3 us
    all_to_all x1, waiting for transfers between devices, shards(): lax.all_to_all(gated, 'ctx', split_axis=1, concat_axis=0, tiled=True)  24.1 us
    all_to_all x1, waiting for transfers between devices, shards(): lax.all_to_all(back.T.astype(jnp.bfloat16), 'ctx', split_axis=0, concat_a...  23.8 us
    reshape x1, local copies, waits for them, and re-layouts, lag_sums(): flat = block.reshape(chan_count, tap_count * span)  17.9 us
    reshape x1, local copies, waits for them, and re-layouts, lag_sums(): skewed = flat.reshape(chan_count, tap_count, span + 1)  17.5 us
    another operation x2, local copies, waits for them, and re-layouts, build_toeplitz(): tiled = jnp.tile(pattern, (1, tap_count))[:, :tap_count * 2 * tap_count]  17.4 us
    ppermute x2, starting transfers between devices, from_behind(): lax.ppermute(value, axis, [(source, source + steps) for source in range(l...  14.1 us
  transfers between devices with their start and end apart: 6, of which 4 were waited for; matrix products, arithmetic and copies ran while one was open for 34% of the time, Pallas kernels for 0%

commit v1 on v0

v1 whole, which is shorter than its diff:
```python
import functools
import math

import jax
import jax.numpy as jnp
import numpy as np
import ml_dtypes
from jax import lax
from jax.experimental import pallas as pl
from jax.experimental.pallas import tpu as pltpu
from jax.sharding import PartitionSpec as P

FL = 128
BINS = 192
N = 2 * BINS
CHUNK = 256
F32 = jnp.float32
BF16 = jnp.bfloat16


def tables():
    k = np.arange(BINS)[:, None]
    fwd, inv = [], []
    for block in range(3):
        u = np.arange(FL)[None, :] + FL * block
        angle = np.pi * ((2 * k + 1) * u % (2 * N)) / N
        full = np.concatenate([np.cos(angle), np.sin(angle)], 0)
        high = full.astype(ml_dtypes.bfloat16)
        low = (full - high.astype(np.float64)).astype(ml_dtypes.bfloat16)
        fwd.append(np.concatenate([high, low], 1))
        zero = np.zeros_like(low.T)
        inv.append(
            np.concatenate(
                [np.concatenate([high.T, high.T], 1), np.concatenate([low.T, zero], 1)], 0
            )
        )
    return np.stack(fwd), np.stack(inv[:2])


def build_matrices(docs, fwd_tab, inv_tab, e_own, e_prev, e_next, d_own):
    own = docs[1:2, :]
    first, last = own[:, :1], own[:, FL - 1 :]
    moved = (own != first).astype(F32)
    split = (first != last).astype(F32)
    keep_prev = (docs[0:1, :] == first).astype(F32)
    keep_next = (docs[2:3, :] == last).astype(F32)
    twice = lambda row: jnp.concatenate([row, row], 1)
    t0, t1, t2 = (fwd_tab[i].astype(F32) for i in range(3))
    m = twice(moved)
    e_own[...] = (t0 * (1.0 - m) + t1 * m).astype(BF16)
    e_prev[...] = (-t2 * twice(keep_prev)).astype(BF16)
    e_next[...] = ((t1 * (1.0 - split) + t2 * split) * twice(keep_next)).astype(BF16)
    square = jnp.broadcast_to(moved, (FL, FL)).T
    wide = jnp.concatenate([square] * (2 * N // FL), 1)
    for half in range(2):
        rows = pl.ds(half * FL, FL)
        d0, d1 = inv_tab[0, rows, :].astype(F32), inv_tab[1, rows, :].astype(F32)
        d_own[rows, :] = (d0 * (1.0 - wide) + d1 * wide).astype(BF16)


def forward(matrix, block):
    return jnp.dot(
        matrix, jnp.concatenate([block, block], 0), preferred_element_type=F32
    )


def inverse(matrix, cosines, sines):
    spectrum = jnp.concatenate([cosines, sines], 0)
    high = spectrum.astype(BF16)
    low = (spectrum - high.astype(F32)).astype(BF16)
    both = jnp.dot(matrix, jnp.concatenate([high, low], 0), preferred_element_type=F32)
    return both[:FL] + both[FL:]


def convolve(a, b):
    ca, sa, cb, sb = a[:BINS], a[BINS:], b[:BINS], b[BINS:]
    return ca * cb - sa * sb, ca * sb + sa * cb


def correlate(a, b):
    ca, sa, cb, sb = a[:BINS], a[BINS:], b[:BINS], b[BINS:]
    return ca * cb + sa * sb, ca * sb - sa * cb


def kernel(docs, fwd_tab, inv_tab, taps, p, p_prev, g, g_next, k_ref, v_ref, o_ref,
           qg_ref, kg_ref, vg_ref, fg_ref, e_own, e_prev, e_next, d_own):
    @pl.when(pl.program_id(0) == 0)
    def _():
        build_matrices(docs[...], fwd_tab, inv_tab, e_own, e_prev, e_next, d_own)

    h_hat = forward(fwd_tab[0], taps[...])
    p_hat = forward(e_own[...], p[...]) + forward(e_prev[...], p_prev[...])
    g_own = forward(e_own[...], g[...])
    g_hat = g_own + forward(e_next[...], g_next[...])
    fg_ref[...] = inverse(inv_tab[0], *correlate(p_hat, g_own)) * (1.0 / BINS)
    mixed = (inverse(d_own[...], *convolve(h_hat, p_hat)) * (1.0 / BINS)).astype(BF16).astype(F32)
    back = (inverse(d_own[...], *correlate(h_hat, g_hat)) * (1.0 / BINS)).astype(BF16).astype(F32)
    qg_ref[...] = (o_ref[...].astype(F32) * mixed).astype(BF16)
    kg_ref[...] = (back * v_ref[...].astype(F32)).astype(BF16)
    vg_ref[...] = (back * k_ref[...].astype(F32)).astype(BF16)


def shards(query_act, key_act, value_act, out_grad, filter_taps, doc_ids):
    rows, chans = key_act.shape
    count = lax.axis_size("dp") * lax.axis_size("ctx")
    scale = 1.0 / math.sqrt(doc_ids.shape[0])
    product = (key_act.astype(F32) * value_act.astype(F32)).astype(BF16)
    gated = (query_act.astype(F32) * out_grad.astype(F32)).astype(BF16)
    p_prev = lax.ppermute(product, ("dp", "ctx"), [(i, i + 1) for i in range(count - 1)])
    g_next = lax.ppermute(gated, ("dp", "ctx"), [(i + 1, i) for i in range(count - 1)])
    taps = lax.all_gather(filter_taps.astype(BF16).T, "ctx", axis=1, tiled=True)
    me = lax.axis_index("dp") * lax.axis_size("ctx") + lax.axis_index("ctx")
    docs = lax.dynamic_slice_in_dim(
        jnp.pad(doc_ids, (FL, FL), constant_values=-1), me * rows, 3 * FL
    ).reshape(3, FL)
    fwd_tab, inv_tab = tables()
    whole = lambda a: pl.BlockSpec(a.shape, lambda i: (0,) * a.ndim)
    part = pl.BlockSpec((FL, CHUNK), lambda i: (0, i))
    acts = jax.ShapeDtypeStruct((FL, chans), BF16)
    query_grad, key_grad, value_grad, partial_grad = pl.pallas_call(
        kernel,
        grid=(chans // CHUNK,),
        in_specs=[whole(docs), whole(fwd_tab), whole(inv_tab)] + [part] * 8,
        out_specs=[part] * 4,
        out_shape=[acts, acts, acts, jax.ShapeDtypeStruct((FL, chans), F32)],
        scratch_shapes=[
            pltpu.VMEM((N, 2 * FL), BF16),
            pltpu.VMEM((N, 2 * FL), BF16),
            pltpu.VMEM((N, 2 * FL), BF16),
            pltpu.VMEM((2 * FL, 2 * N), BF16),
        ],
        name="mixer",
    )(docs, jnp.asarray(fwd_tab), jnp.asarray(inv_tab), taps, product, p_prev, gated, g_next,
      key_act, value_act, out_grad)
    partial_grad = lax.psum_scatter(partial_grad, "ctx", scatter_dimension=1, tiled=True)
    total = lax.psum(partial_grad, "dp")
    return query_grad, key_grad, value_grad, total.T * scale


def solution(mesh):
    act = P(("dp", "ctx"), None)
    return jax.shard_map(
        shards,
        mesh=mesh,
        in_specs=(act, act, act, act, P("ctx", None), P()),
        out_specs=(act, act, act, P("ctx", None)),
        check_vma=False,
    )
```

time: 371 us -> 403 us (1.086)
  waiting for transfers between devices: 110 us -> 347 us
  local copies, waits for them, and re-layouts: 117 us -> 3.06 us
  matrix products: 44.3 us -> 0 us
  blocking collectives: 31.3 us -> 0 us
  starting transfers between devices: 35.9 us -> 13.2 us
  Pallas kernels: 0 us -> 20.4 us
  other arithmetic: 14.7 us -> 2.99 us
    reduce_scatter x0 -> x1, waiting for transfers between devices: none -> 215 us  [shards(): lax.psum_scatter(partial_grad, 'ctx', scatter_dimension=1, tiled=True)]
    reshape x4 -> x1, local copies, waits for them, and re-layouts: 49.4 us -> 0.67 us  [shards(): docs = lax.dynamic_slice_in_dim(jnp.pad(doc_ids, (FL, FL), constant_value...]
    all_to_all x3 -> x0, waiting for transfers between devices: 47.9 us -> none  [the longest x1 24.1 us: shards(): lax.all_to_all(gated, 'ctx', split_axis=1, concat_axis=0, tiled=True)]
    dot_general x6 -> x0, matrix products: 44.3 us -> none  [the longest x1 14 us: mix_block(): jnp.einsum('cbi,cbj->cij', g_other[:, :block_count], kv_other, preferred_...]
    all_gather x0 -> x1, waiting for transfers between devices: none -> 42.9 us  [shards(): taps = lax.all_gather(filter_taps.astype(BF16).T, 'ctx', axis=1, tiled=True)]
    all_to_all x1 -> x0, blocking collectives: 31.3 us -> none  [shards(): lax.all_to_all(product, 'ctx', split_axis=1, concat_axis=0, tiled=True)]
    all_to_all x3 -> x0, starting transfers between devices: 21.5 us -> none  [the longest x1 11.9 us: shards(): lax.all_to_all(gated, 'ctx', split_axis=1, concat_axis=0, tiled=True)]
    pallas_call x0 -> x1, Pallas kernels: none -> 20.4 us  [shards(): pl.pallas_call(kernel, grid=(chans // CHUNK,), in_specs=[whole(docs), who...]
  transfers between devices with their start and end apart: 6 -> 5, of which waited for: 4 -> 4; matrix products, arithmetic and copies ran while one was open for 34% -> 1% of each run, Pallas kernels for 0% -> 0%
where the time goes in v1:
time: 403 us; the launch traced here: 400 us
  waiting for transfers between devices  347 us (86%)
  Pallas kernels  20.4 us (5%)
  between operations  13.9 us (3%)
  starting transfers between devices  13.2 us (3%)
    reduce_scatter x1, waiting for transfers between devices, shards(): lax.psum_scatter(partial_grad, 'ctx', scatter_dimension=1, tiled=True)  215 us
    psum x1, waiting for transfers between devices, shards(): total = lax.psum(partial_grad, 'dp')  67.8 us
    all_gather x1, waiting for transfers between devices, shards(): taps = lax.all_gather(filter_taps.astype(BF16).T, 'ctx', axis=1, tiled=True)  42.9 us
    ppermute x1, waiting for transfers between devices, shards(): lax.ppermute(product, ('dp', 'ctx'), [(i, i + 1) for i in range(count - 1)])  20.9 us
    pallas_call x1, Pallas kernels, shards(): pl.pallas_call(kernel, grid=(chans // CHUNK,), in_specs=[whole(docs), who...  20.4 us
    ppermute x1, starting transfers between devices, shards(): lax.ppermute(gated, ('dp', 'ctx'), [(i + 1, i) for i in range(count - 1)])  8.58 us
  transfers between devices with their start and end apart: 5, of which 4 were waited for; matrix products, arithmetic and copies ran while one was open for 1% of the time, Pallas kernels for 0%

profile of v1, /device:TPU:1, one launch (start us, length us, event | category | flops | bytes accessed | tf_op | source)
XLA Modules:
  0.0 400.3 jit_solution(2416178335702163490)
XLA Ops:
  7.2 0.0 copy-start
  7.2 0.0 all-gather.2.cloned.1.call-start
  7.2 1.6 copy.12
  8.9 0.0 all-gather.2.cloned.1.call-update
  8.9 0.0 reduce-scatter.2.cloned.1.call-start
  8.9 0.0 copy-start.3
  8.9 1.9 multiply_convert_fusion.1.p
  10.8 0.0 copy-start.5
  10.8 4.5 %collective-permute-start = (bf16[128,4096]{1,0:T(8,128)(2,1)S(1)}, bf16[128,4096]{1,0:T(8,128)(2,1)}, u32[]{:S(2)}, u32[]{:S(2)}) collective-permute-start(bf16[128,4096]{1,0:T(8,128)(2,1)S(1)} %multiply_convert_fusion.1.p), channel_id=1, source_target_pairs={{0,1},{1,2},{2,3},{3,4},{4,5},{5,6},{6,7},{7,8},{8,9},{9,10},{10,1... | collective-permute-start | bytes 3145736 | tf_op jit(solution)/shard_map/ppermute | solution.py:109
  15.4 0.3 multiply_convert_fusion.g
  15.7 8.6 %collective-permute-start.1 = (bf16[128,4096]{1,0:T(8,128)(2,1)S(1)}, bf16[128,4096]{1,0:T(8,128)(2,1)S(1)}, u32[]{:S(2)}, u32[]{:S(2)}) collective-permute-start(bf16[128,4096]{1,0:T(8,128)(2,1)S(1)} %multiply_convert_fusion.g), channel_id=1, source_target_pairs={{1,0},{2,1},{3,2},{4,3},{5,4},{6,5},{7,6},{8,7},{9,8},{10,9},{11,1... | collective-permute-start | bytes 3145736 | tf_op jit(solution)/shard_map/ppermute | solution.py:110
  24.3 0.7 fusion.docs
  25.0 20.9 %collective-permute-done.p_prev = bf16[128,4096]{1,0:T(8,128)(2,1)} collective-permute-done((bf16[128,4096]{1,0:T(8,128)(2,1)S(1)}, bf16[128,4096]{1,0:T(8,128)(2,1)}, u32[]{:S(2)}, u32[]{:S(2)}) %collective-permute-start) | collective-permute-done | bytes 1048608 | tf_op jit(solution)/shard_map/ppermute | solution.py:109
  45.8 0.0 collective-permute-done.1.g_next
  45.8 42.9 %all-gather.2.cloned.1.call-done.taps = bf16[128,4096]{1,0:T(8,128)(2,1)} async-done(((bf16[128,128]{1,0:T(8,128)(2,1)}), bf16[128,4096]{1,0:T(8,128)(2,1)}) %all-gather.2.cloned.1.call-update) | async-done | bytes 1048592 | tf_op jit(solution)/shard_map/all_gather | solution.py:111
  88.8 0.0 copy-done.4
  88.8 20.4 %mixer.1 = (bf16[128,4096]{1,0:T(8,128)(2,1)}, bf16[128,4096]{1,0:T(8,128)(2,1)}, bf16[128,4096]{1,0:T(8,128)(2,1)}, f32[128,4096]{1,0:T(8,128)}) custom-call(s32[3,128]{1,0:T(4,128)} %fusion.docs, bf16[3,384,256]{2,1,0:T(8,128)(2,1)} %constant.25.clone.fwd_tab, bf16[2,256,768]{2,1,0:T(8,128)(2,1)} %constant.26.clone.inv_tab, ...), custom_call_target="tpu_custom_call" | custom-call | tf_op jit(solution)/shard_map/mixer/pallas_call | solution.py:120
  109.2 0.0 reduce-scatter.2.cloned.1.call-update
  109.2 0.0 all-reduce.3.cloned.1.call-start
  109.2 215.2 %reduce-scatter.2.cloned.1.call-done = f32[128,128]{1,0:T(8,128)} async-done(((f32[128,4096]{1,0:T(8,128)}), f32[128,128]{1,0:T(8,128)}) %reduce-scatter.2.cloned.1.call-update) | async-done | bytes 65552 | tf_op jit(solution)/shard_map/reduce_scatter | solution.py:135
  324.4 0.0 all-reduce.3.cloned.1.call-update
  324.4 67.8 %all-reduce.3.cloned.1.call-done = f32[128,128]{1,0:T(8,128)} async-done(((f32[128,128]{1,0:T(8,128)}), f32[128,128]{1,0:T(8,128)}) %all-reduce.3.cloned.1.call-update) | async-done | bytes 65552 | tf_op jit(solution)/shard_map/psum | solution.py:136
  392.2 0.8 multiply_bitcast_fusion
  393.1 0.7 copy.13
  (8 shorter events, 0.0 us)
Async XLA Ops:
  7.2 8.2 %copy-start = (bf16[128,4096]{1,0:T(8,128)(2,1)S(1)}, bf16[128,4096]{1,0:T(8,128)(2,1)}, u32[]{:S(2)}) copy-start(bf16[128,4096]{1,0:T(8,128)(2,1)} %o_ref.1) | copy-start | bytes 3145732
  7.2 81.6 %all-gather.2.cloned.1.call-start = ((), (), s32[]{:S(2)}) async-start(), calls=%async_computation.1 | async-start | bytes 1081344 | tf_op jit(solution)/shard_map/all_gather | solution.py:111
  8.9 315.5 %reduce-scatter.2.cloned.1.call-start = ((), (), s32[]{:S(2)}) async-start(), calls=%async_computation.2 | async-start | bytes 2162688 | tf_op jit(solution)/shard_map/reduce_scatter | solution.py:135
  8.9 6.5 %copy-start.3 = (bf16[128,4096]{1,0:T(8,128)(2,1)S(1)}, bf16[128,4096]{1,0:T(8,128)(2,1)}, u32[]{:S(2)}) copy-start(bf16[128,4096]{1,0:T(8,128)(2,1)} %param.8) | copy-start | bytes 3145732
  10.8 77.9 %copy-start.1 = (bf16[128,4096]{1,0:T(8,128)(2,1)}, bf16[128,4096]{1,0:T(8,128)(2,1)S(1)}, u32[]{:S(2)}) copy-start(bf16[128,4096]{1,0:T(8,128)(2,1)S(1)} %multiply_convert_fusion.1.p) | copy-start | bytes 3145732
  10.8 13.5 %copy-start.5 = (s32[32768]{0:T(1024)S(1)}, s32[32768]{0:T(1024)}, u32[]{:S(2)}) copy-start(s32[32768]{0:T(1024)} %param.13) | copy-start | bytes 393220
  10.8 35.0 %collective-permute-start = (bf16[128,4096]{1,0:T(8,128)(2,1)S(1)}, bf16[128,4096]{1,0:T(8,128)(2,1)}, u32[]{:S(2)}, u32[]{:S(2)}) collective-permute-start(bf16[128,4096]{1,0:T(8,128)(2,1)S(1)} %multiply_convert_fusion.1.p), channel_id=1, source_target_pairs={{0,1},{1,2},{2,3},{3,4},{4,5},{5,6},{6,7},{7,8},{8,9},{9,10},{10,1... | collective-permute-start | bytes 3145736 | tf_op jit(solution)/shard_map/ppermute | solution.py:109
  15.7 73.1 %copy-start.2 = (bf16[128,4096]{1,0:T(8,128)(2,1)}, bf16[128,4096]{1,0:T(8,128)(2,1)S(1)}, u32[]{:S(2)}) copy-start(bf16[128,4096]{1,0:T(8,128)(2,1)S(1)} %multiply_convert_fusion.g) | copy-start | bytes 3145732
  15.7 30.1 %collective-permute-start.1 = (bf16[128,4096]{1,0:T(8,128)(2,1)S(1)}, bf16[128,4096]{1,0:T(8,128)(2,1)S(1)}, u32[]{:S(2)}, u32[]{:S(2)}) collective-permute-start(bf16[128,4096]{1,0:T(8,128)(2,1)S(1)} %multiply_convert_fusion.g), channel_id=1, source_target_pairs={{1,0},{2,1},{3,2},{4,3},{5,4},{6,5},{7,6},{8,7},{9,8},{10,9},{11,1... | collective-permute-start | bytes 3145736 | tf_op jit(solution)/shard_map/ppermute | solution.py:110
  45.8 42.9 %copy-start.4 = (bf16[128,4096]{1,0:T(8,128)(2,1)}, bf16[128,4096]{1,0:T(8,128)(2,1)S(1)}, u32[]{:S(2)}) copy-start(bf16[128,4096]{1,0:T(8,128)(2,1)S(1)} %collective-permute-done.1.g_next) | copy-start | bytes 3145732
  109.2 283.0 %all-reduce.3.cloned.1.call-start = ((), (), s32[]{:S(2)}) async-start(), calls=%async_computation.3 | async-start | bytes 131072 | tf_op jit(solution)/shard_map/psum | solution.py:136
Sparse Core Ops, SparseCore 0:
  11.0 77.6 all-gather.1
  109.3 215.0 reduce-scatter.1
  326.8 65.3 all-reduce.2

commit v2 on v1

v2 whole, which is shorter than its diff:
```python
import functools
import math

import jax
import jax.numpy as jnp
import numpy as np
import ml_dtypes
from jax import lax
from jax.experimental import pallas as pl
from jax.experimental.pallas import tpu as pltpu
from jax.sharding import PartitionSpec as P

FL = 128
BINS = 192
N = 2 * BINS
CHUNK = 256
F32 = jnp.float32
BF16 = jnp.bfloat16


def tables():
    k = np.arange(BINS)[:, None]
    fwd, inv = [], []
    for block in range(3):
        u = np.arange(FL)[None, :] + FL * block
        angle = np.pi * ((2 * k + 1) * u % (2 * N)) / N
        full = np.concatenate([np.cos(angle), np.sin(angle)], 0)
        high = full.astype(ml_dtypes.bfloat16)
        low = (full - high.astype(np.float64)).astype(ml_dtypes.bfloat16)
        fwd.append(np.concatenate([high, low], 1))
        zero = np.zeros_like(low.T)
        inv.append(
            np.concatenate(
                [np.concatenate([high.T, high.T], 1), np.concatenate([low.T, zero], 1)], 0
            )
        )
    return np.stack(fwd), np.stack(inv[:2])


def forward(matrix, block):
    return jnp.dot(
        matrix, jnp.concatenate([block, block], 0), preferred_element_type=F32
    )


def inverse(matrix, cosines, sines):
    spectrum = jnp.concatenate([cosines, sines], 0)
    high = spectrum.astype(BF16)
    low = (spectrum - high.astype(F32)).astype(BF16)
    both = jnp.dot(matrix, jnp.concatenate([high, low], 0), preferred_element_type=F32)
    return both[:FL] + both[FL:]


def convolve(a, b):
    ca, sa, cb, sb = a[:BINS], a[BINS:], b[:BINS], b[BINS:]
    return ca * cb - sa * sb, ca * sb + sa * cb


def correlate(a, b):
    ca, sa, cb, sb = a[:BINS], a[BINS:], b[:BINS], b[BINS:]
    return ca * cb + sa * sb, ca * sb - sa * cb

MESH = pl.DeviceIdType.MESH


class Layout:
    def __init__(self, dp, ctx, chans, chunk=CHUNK):
        self.dp, self.ctx, self.cores, self.ys = dp, ctx, 2, dp // 2
        self.zs = 8 if ctx == 32 else ctx // 2
        self.xs = ctx // self.zs
        self.chans, self.chunk = chans, chunk
        self.chunks = chans // chunk
        self.half = self.chunks // 2
        self.group = self.chunks // self.xs
        self.rows = FL // dp
        self.lanes = chans // ctx
        self.ahead = min(3, self.half)


def remote(src, dst, send, recv, device):
    return pltpu.make_async_remote_copy(
        src_ref=src, dst_ref=dst, send_sem=send, recv_sem=recv, device_id=device,
        device_id_type=MESH,
    )


def kernel(lay, scale, q_hbm, k_hbm, v_hbm, o_hbm, taps, docs, fwd_tab, inv_tab,
           qg_ref, kg_ref, vg_ref, fg_ref,
           q, k, v, o, p, g, p_prev, g_next, pa_hat, ga_hat, pb_hat, gb_hat,
           e_own, e_prev, e_next, d_own, tap_own, tap_all, fg_part, c_recv, y_send, y_recv,
           x_send, x_recv, z_send, z_recv, final,
           in_sem, p_ssem, p_rsem, g_ssem, g_rsem, tz_ssem, tz_rsem, tx_ssem, tx_rsem,
           ty_ssem, ty_rsem, tc_ssem, tc_rsem, c_ssem, c_rsem, y_ssem, y_rsem,
           x_ssem, x_rsem, z_ssem, z_rsem, f_ssem, f_rsem):
    dp, ctx = lax.axis_index("dp"), lax.axis_index("ctx")
    DP, CTX, X, Y, Z = lay.dp, lay.ctx, lay.xs, lay.ys, lay.zs
    NC, HALF, GC, CH = lay.chunks, lay.half, lay.group, lay.chunk
    y, core = lax.div(dp, 2), lax.rem(dp, 2)
    x, z = lax.div(ctx, Z), lax.rem(ctx, Z)
    me = dp * CTX + ctx
    after, before = lax.rem(me + 1, DP * CTX), lax.rem(me + DP * CTX - 1, DP * CTX)
    place = lambda flat: (lax.div(flat, CTX), lax.rem(flat, CTX))
    nxt, prv = place(after), place(before)
    z_peer = lambda r: (dp, x * Z + lax.rem(z + r, Z))
    x_peer = lambda r: (dp, lax.rem(x + r, X) * Z + z)
    y_peer = lambda r: (2 * lax.rem(y + r, Y) + core, ctx)
    d_peer = lambda r: (lax.rem(dp + r, DP), ctx)
    partner = (2 * y + 1 - core, ctx)
    slot = core * Y + y

    barrier = pltpu.get_barrier_semaphore()
    peers = [nxt, prv] + [z_peer(r) for r in range(1, Z)]
    peers += [x_peer(r) for r in range(1, X)] + [d_peer(r) for r in range(1, DP)]
    for peer in peers:
        pl.semaphore_signal(barrier, inc=1, device_id=peer, device_id_type=MESH)

    def load(which, n):
        hbm, ref = ((q_hbm, q), (k_hbm, k), (v_hbm, v), (o_hbm, o))[which]
        return pltpu.make_async_copy(
            hbm.at[:, pl.ds(pl.multiple_of(n * CH, CH), CH)], ref.at[n], in_sem.at[which, n]
        )

    def start_loads(j, carry):
        for which, n in ((1, j), (2, j), (0, j + HALF), (3, j + HALF),
                         (1, j + HALF), (2, j + HALF), (0, j), (3, j)):
            load(which, n).start()
        return carry

    lax.fori_loop(0, HALF, start_loads, 0)

    turned = taps[...].T.astype(BF16)
    tap_own[...] = turned.reshape(DP, lay.rows, lay.lanes)
    tap_all[slot, ctx] = tap_own[slot]

    above, below = jnp.maximum(me - 1, 0), jnp.minimum(me + 1, DP * CTX - 1)
    own = docs[pl.ds(me, 1), :]
    first, last = own[:, :1], own[:, FL - 1 :]
    moved = (own != first).astype(F32)
    split = (first != last).astype(F32)
    keep_prev = (docs[pl.ds(above, 1), :] == first).astype(F32) * (me > 0).astype(F32)
    keep_next = (docs[pl.ds(below, 1), :] == last).astype(F32) * (me < DP * CTX - 1).astype(F32)
    twice = lambda row: jnp.concatenate([row, row], 1)
    t0, t1, t2 = (fwd_tab[i].astype(F32) for i in range(3))
    m = twice(moved)
    e_own[...] = (t0 * (1.0 - m) + t1 * m).astype(BF16)
    e_prev[...] = (-t2 * twice(keep_prev)).astype(BF16)
    e_next[...] = ((t1 * (1.0 - split) + t2 * split) * twice(keep_next)).astype(BF16)
    square = jnp.broadcast_to(moved, (FL, FL)).T
    wide = jnp.concatenate([square] * (2 * N // FL), 1)
    for half in range(2):
        rows = pl.ds(half * FL, FL)
        d0, d1 = inv_tab[0, rows, :].astype(F32), inv_tab[1, rows, :].astype(F32)
        d_own[rows, :] = (d0 * (1.0 - wide) + d1 * wide).astype(BF16)

    def tap_z(r):
        here = tap_all.at[slot, ctx]
        return remote(here, here, tz_ssem.at[r - 1], tz_rsem.at[r - 1], z_peer(r))

    def tap_x(r):
        here = tap_all.at[slot, pl.ds(x * Z, Z)]
        return remote(here, here, tx_ssem.at[r - 1], tx_rsem.at[r - 1], x_peer(r))

    def tap_y(r):
        here = tap_all.at[slot]
        return remote(here, here, ty_ssem.at[r - 1], ty_rsem.at[r - 1], y_peer(r))

    def tap_c():
        here = tap_all.at[pl.ds(core * Y, Y)]
        return remote(here, here, tc_ssem, tc_rsem, partner)

    def halo_p(n):
        return remote(p.at[n], p_prev.at[n], p_ssem.at[n], p_rsem.at[n], nxt)

    def halo_g(n):
        return remote(g.at[n], g_next.at[n], g_ssem.at[n], g_rsem.at[n], prv)

    def pair(n):
        return remote(fg_part.at[n, 1 - core], c_recv.at[n], c_ssem.at[n], c_rsem.at[n], partner)

    def part_y(r, group):
        chunks = pl.ds(group * GC, GC)
        return remote(y_send.at[lax.rem(y + r, Y), chunks], y_recv.at[r - 1, chunks],
                      y_ssem.at[r - 1, group], y_rsem.at[r - 1, group], y_peer(r))

    def part_x(r):
        return remote(x_send.at[pl.ds(lax.rem(x + r, X) * GC, GC)], x_recv.at[r - 1],
                      x_ssem.at[r - 1], x_rsem.at[r - 1], x_peer(r))

    def part_z(r):
        return remote(z_send.at[lax.rem(z + r, Z)], z_recv.at[r - 1],
                      z_ssem.at[r - 1], z_rsem.at[r - 1], z_peer(r))

    def part_f(r):
        here = final.at[slot]
        return remote(here, here, f_ssem.at[r - 1], f_rsem.at[r - 1], d_peer(r))

    def produce(j):
        for n in (j, j + HALF):
            load(1, n).wait()
            load(2, n).wait()
            p[n] = (k[n].astype(F32) * v[n].astype(F32)).astype(BF16)
            load(0, n).wait()
            load(3, n).wait()
            g[n] = (q[n].astype(F32) * o[n].astype(F32)).astype(BF16)

    def send(n):
        halo_p(n).start()
        halo_g(lax.rem(n + HALF, NC)).start()

    def produce_and_send(j, carry):
        produce(j)
        send(j)
        return carry

    produce(0)
    pl.semaphore_wait(barrier, len(peers))
    for r in range(1, Z):
        tap_z(r).start()
    send(0)
    lax.fori_loop(1, lay.ahead, produce_and_send, 0)

    def absorb(n):
        pair(n).wait_recv()
        y_send[:, n] = (fg_part[n, core] + c_recv[n]).reshape(Y, lay.rows, CH)

    def send_groups(gi):
        for group in (gi, gi + X // 2):
            for r in range(1, Y):
                part_y(r, group).start()

    def relay_x():
        for r in range(1, Z):
            tap_z(r).wait_recv()
        for r in range(1, X):
            tap_x(r).start()

    def relay_y():
        for r in range(1, X):
            tap_x(r).wait_recv()
        for r in range(1, Y):
            tap_y(r).start()

    def relay_c():
        for r in range(1, Y):
            tap_y(r).wait_recv()
        tap_c().start()

    def sum_y():
        for r in range(1, Y):
            for group in range(X):
                part_y(r, group).wait_recv()
        total = y_send[y]
        for r in range(1, Y):
            total = total + y_recv[r - 1]
        x_send[...] = total
        for r in range(1, X):
            part_x(r).start()

    def sum_x():
        for r in range(1, X):
            part_x(r).wait_recv()
        total = x_send[pl.ds(x * GC, GC)]
        for r in range(1, X):
            total = total + x_recv[r - 1]
        per = CH // lay.lanes
        for i in range(Z):
            lane = (i % per) * lay.lanes
            z_send[i] = total[i // per, :, lane : lane + lay.lanes]
        for r in range(1, Z):
            part_z(r).start()

    def sum_z():
        for r in range(1, Z):
            part_z(r).wait_recv()
        total = z_send[z]
        for r in range(1, Z):
            total = total + z_recv[r - 1]
        final[slot] = total
        for r in range(1, DP):
            part_f(r).start()

    def scheduled(j, events):
        for step, event in events:
            if step < HALF:
                pl.when(j == step)(event)

    early = ((1, relay_x), (3, relay_y), (6, relay_c))
    late = ((2, sum_y), (4, sum_x), (6, sum_z))

    def first_half(j, carry):
        @pl.when(j + lay.ahead < HALF)
        def _():
            produce(j + lay.ahead)

        @pl.when(j + lay.ahead < NC)
        def _():
            send(j + lay.ahead)

        scheduled(j, early)
        a, b = j, j + HALF
        ga = forward(e_own[...], g[a])
        pb = forward(e_own[...], p[b])
        ga_hat[j] = ga
        pb_hat[j] = pb
        pa = forward(e_own[...], p[a])
        halo_p(a).wait_recv()
        pa = pa + forward(e_prev[...], p_prev[a])
        pa_hat[j] = pa
        fg_part[a] = inverse(inv_tab[0], *correlate(pa, ga)).reshape(2, FL // 2, CH)
        pair(a).start()
        gb = forward(e_own[...], g[b])
        halo_g(b).wait_recv()
        gb = gb + forward(e_next[...], g_next[b])
        gb_hat[j] = gb
        fg_part[b] = inverse(inv_tab[0], *correlate(pb, gb)).reshape(2, FL // 2, CH)
        pair(b).start()

        @pl.when(j > 0)
        def _():
            absorb(j - 1)
            absorb(j - 1 + HALF)

        @pl.when((j > 0) & (lax.rem(j, GC) == 0))
        def _():
            send_groups(lax.div(j, GC) - 1)

        return carry

    lax.fori_loop(0, HALF, first_half, 0)
    for step, event in early:
        if step >= HALF:
            event()
    absorb(HALF - 1)
    absorb(NC - 1)
    send_groups(HALF // GC - 1)
    tap_c().wait_recv()

    def taps_of(n):
        per = CH // lay.lanes
        return jnp.concatenate(
            [tap_all[:, n * per + i].reshape(FL, lay.lanes) for i in range(per)], 1
        )

    def rounded(value):
        return (value * (1.0 / BINS)).astype(BF16).astype(F32)

    def write_query(n, mixed):
        cols = pl.ds(pl.multiple_of(n * CH, CH), CH)
        qg_ref[:, cols] = (o[n].astype(F32) * mixed).astype(BF16)

    def write_kv(n, back):
        cols = pl.ds(pl.multiple_of(n * CH, CH), CH)
        kg_ref[:, cols] = (back * v[n].astype(F32)).astype(BF16)
        vg_ref[:, cols] = (back * k[n].astype(F32)).astype(BF16)

    def second_half(j, carry):
        @pl.when(j + HALF + lay.ahead < NC)
        def _():
            send(j + HALF + lay.ahead)

        scheduled(j, late)
        a, b = j, j + HALF
        ha = forward(fwd_tab[0], taps_of(a))
        write_query(a, rounded(inverse(d_own[...], *convolve(ha, pa_hat[j]))))
        hb = forward(fwd_tab[0], taps_of(b))
        write_kv(b, rounded(inverse(d_own[...], *correlate(hb, gb_hat[j]))))
        halo_g(a).wait_recv()
        ga = ga_hat[j] + forward(e_next[...], g_next[a])
        write_kv(a, rounded(inverse(d_own[...], *correlate(ha, ga))))
        halo_p(b).wait_recv()
        pb = pb_hat[j] + forward(e_prev[...], p_prev[b])
        write_query(b, rounded(inverse(d_own[...], *convolve(hb, pb))))
        return carry

    lax.fori_loop(0, HALF, second_half, 0)
    for step, event in late:
        if step >= HALF:
            event()
    for r in range(1, DP):
        part_f(r).wait_recv()
    fg_ref[...] = final[...].reshape(FL, lay.lanes).T * (scale / BINS)

    def drain(n, carry):
        halo_p(n).wait_send()
        halo_g(n).wait_send()
        pair(n).wait_send()
        return carry

    lax.fori_loop(0, NC, drain, 0)
    for r in range(1, Z):
        tap_z(r).wait_send()
        part_z(r).wait_send()
    for r in range(1, X):
        tap_x(r).wait_send()
        part_x(r).wait_send()
    for r in range(1, Y):
        tap_y(r).wait_send()
        for group in range(X):
            part_y(r, group).wait_send()
    for r in range(1, DP):
        part_f(r).wait_send()
    tap_c().wait_send()


def shards(query_act, key_act, value_act, out_grad, filter_taps, doc_ids):
    rows, chans = key_act.shape
    lay = Layout(lax.axis_size("dp"), lax.axis_size("ctx"), chans)
    scale = 1.0 / math.sqrt(doc_ids.shape[0])
    fwd_tab, inv_tab = tables()
    acts = jax.ShapeDtypeStruct((rows, chans), BF16)
    any_spec, vmem = pl.BlockSpec(memory_space=pl.ANY), pl.BlockSpec(memory_space=pltpu.VMEM)
    NC, CH, GC, DP, X, Y, Z = (
        lay.chunks, lay.chunk, lay.group, lay.dp, lay.xs, lay.ys, lay.zs
    )
    block = pltpu.VMEM((NC, FL, CH), BF16)
    spectra = pltpu.VMEM((lay.half, N, CH), F32)
    mat = pltpu.VMEM((N, 2 * FL), BF16)
    dma = pltpu.SemaphoreType.DMA
    return pl.pallas_call(
        functools.partial(kernel, lay, scale),
        in_specs=[any_spec] * 4 + [vmem] * 4,
        out_specs=[vmem] * 4,
        out_shape=[acts, acts, acts, jax.ShapeDtypeStruct(filter_taps.shape, F32)],
        scratch_shapes=[block] * 8 + [spectra] * 4 + [
            mat, mat, mat,
            pltpu.VMEM((2 * FL, 2 * N), BF16),
            pltpu.VMEM((DP, lay.rows, lay.lanes), BF16),
            pltpu.VMEM((DP, lay.ctx, lay.rows, lay.lanes), BF16),
            pltpu.VMEM((NC, 2, FL // 2, CH), F32),
            pltpu.VMEM((NC, FL // 2, CH), F32),
            pltpu.VMEM((Y, NC, lay.rows, CH), F32),
            pltpu.VMEM((Y - 1, NC, lay.rows, CH), F32),
            pltpu.VMEM((NC, lay.rows, CH), F32),
            pltpu.VMEM((X - 1, GC, lay.rows, CH), F32),
            pltpu.VMEM((Z, lay.rows, lay.lanes), F32),
            pltpu.VMEM((Z - 1, lay.rows, lay.lanes), F32),
            pltpu.VMEM((DP, lay.rows, lay.lanes), F32),
            dma((4, NC)), dma((NC,)), dma((NC,)), dma((NC,)), dma((NC,)),
            dma((Z - 1,)), dma((Z - 1,)), dma((X - 1,)), dma((X - 1,)),
            dma((Y - 1,)), dma((Y - 1,)), dma, dma, dma((NC,)), dma((NC,)),
            dma((Y - 1, X)), dma((Y - 1, X)), dma((X - 1,)), dma((X - 1,)),
            dma((Z - 1,)), dma((Z - 1,)), dma((DP - 1,)), dma((DP - 1,)),
        ],
        compiler_params=pltpu.CompilerParams(
            collective_id=0, has_side_effects=True, vmem_limit_bytes=60 * 2**20
        ),
        name="mixer",
    )(query_act, key_act, value_act, out_grad, filter_taps,
      doc_ids.reshape(-1, FL), jnp.asarray(fwd_tab), jnp.asarray(inv_tab))


def solution(mesh):
    act = P(("dp", "ctx"), None)
    return jax.shard_map(
        shards,
        mesh=mesh,
        in_specs=(act, act, act, act, P("ctx", None), P()),
        out_specs=(act, act, act, P("ctx", None)),
        check_vma=False,
    )
```

time: 403 us -> 74.8 us (0.19)
  the two profiles are of different devices: /device:TPU:1 before, /device:TPU:5 now
where the time goes in v2:
time: 74.8 us; the launch traced here: 74.6 us
  Pallas kernels  68.4 us (91%)
  local copies, waits for them, and re-layouts  5.58 us (7%)
    pallas_call x1, Pallas kernels, shards(): pl.pallas_call(functools.partial(kernel, lay, scale), in_specs=[any_spec]...  68.4 us
    unnamed x10, local copies, waits for them, and re-layouts  5.58 us

profile of v2, /device:TPU:5, one launch (start us, length us, event | category | flops | bytes accessed | tf_op | source)
XLA Modules:
  0.0 74.6 jit_solution(17735830537156224782)
XLA Ops:
  0.6 68.4 %mixer.1 = (bf16[128,4096]{1,0:T(8,128)(2,1)}, bf16[128,4096]{1,0:T(8,128)(2,1)}, bf16[128,4096]{1,0:T(8,128)(2,1)}, f32[128,128]{1,0:T(8,128)}) custom-call(bf16[128,4096]{1,0:T(8,128)(2,1)} %q_hbm.1, bf16[128,4096]{1,0:T(8,128)(2,1)} %k_hbm.1, bf16[128,4096]{1,0:T(8,128)(2,1)} %v_hbm.1, bf16[128,4096]{1,0:T(8,128)(2,1)} %o_hbm.1, f32[128,128]{1,0:T(8,128)} %taps.1, ...), custom_call_target="tpu_custom_call" | custom-call | tf_op jit(solution)/shard_map/mixer/pallas_call | solution.py:419
  69.0 0.0 copy-start.1
  69.0 2.4 %copy.16 = bf16[128,4096]{1,0:T(8,128)(2,1)} copy(bf16[128,4096]{1,0:T(8,128)(2,1)} %get-tuple-element.8) | data formatting | bytes 2097152
  71.4 0.0 copy-done.1
  71.4 0.0 copy-start
  71.4 1.0 %copy.17 = bf16[128,4096]{1,0:T(8,128)(2,1)} copy(bf16[128,4096]{1,0:T(8,128)(2,1)S(1)} %copy-done.1) | data formatting | bytes 2097152
  72.4 0.6 copy-done
  73.0 0.0 copy-start.2
  73.0 1.0 %copy.18 = bf16[128,4096]{1,0:T(8,128)(2,1)} copy(bf16[128,4096]{1,0:T(8,128)(2,1)S(1)} %copy-done) | data formatting | bytes 2097152
  74.0 0.0 copy-done.2
  74.0 0.6 copy.19
Async XLA Ops:
  69.0 2.4 %copy-start.1 = (bf16[128,4096]{1,0:T(8,128)(2,1)S(1)}, bf16[128,4096]{1,0:T(8,128)(2,1)}, u32[]{:S(2)}) copy-start(bf16[128,4096]{1,0:T(8,128)(2,1)} %get-tuple-element.9) | copy-start | bytes 3145732
  71.4 1.6 %copy-start = (bf16[128,4096]{1,0:T(8,128)(2,1)S(1)}, bf16[128,4096]{1,0:T(8,128)(2,1)}, u32[]{:S(2)}) copy-start(bf16[128,4096]{1,0:T(8,128)(2,1)} %get-tuple-element.10) | copy-start | bytes 3145732
  73.0 1.0 %copy-start.2 = (f32[128,128]{1,0:T(8,128)S(1)}, f32[128,128]{1,0:T(8,128)}, u32[]{:S(2)}) copy-start(f32[128,128]{1,0:T(8,128)} %get-tuple-element.11) | copy-start | bytes 196612

commit v3 on v2

--- a/solution.py
+++ b/solution.py
@@ -74,7 +74,6 @@
         self.group = self.chunks // self.xs
         self.rows = FL // dp
         self.lanes = chans // ctx
-        self.ahead = min(3, self.half)
 
 
 def remote(src, dst, send, recv, device):
@@ -84,8 +83,8 @@
     )
 
 
-def kernel(lay, scale, q_hbm, k_hbm, v_hbm, o_hbm, taps, docs, fwd_tab, inv_tab,
-           qg_ref, kg_ref, vg_ref, fg_ref,
+def kernel(lay, q_hbm, k_hbm, v_hbm, o_hbm, taps, docs, fwd_tab, inv_tab,
+           mixed_ref, back_ref, fg_ref,
            q, k, v, o, p, g, p_prev, g_next, pa_hat, ga_hat, pb_hat, gb_hat,
            e_own, e_prev, e_next, d_own, tap_own, tap_all, fg_part, c_recv, y_send, y_recv,
            x_send, x_recv, z_send, z_recv, final,
@@ -212,16 +211,21 @@
         send(j)
         return carry
 
+    def send_rest(n, carry):
+        send(n)
+        return carry
+
     produce(0)
     pl.semaphore_wait(barrier, len(peers))
     for r in range(1, Z):
         tap_z(r).start()
     send(0)
-    lax.fori_loop(1, lay.ahead, produce_and_send, 0)
+    lax.fori_loop(1, HALF, produce_and_send, 0)
+    lax.fori_loop(HALF, NC, send_rest, 0)
 
     def absorb(n):
         pair(n).wait_recv()
-        y_send[:, n] = (fg_part[n, core] + c_recv[n]).reshape(Y, lay.rows, CH)
+        y_send[:, n] = (fg_part[n, core] + c_recv[n]).astype(BF16)
 
     def send_groups(gi):
         for group in (gi, gi + X // 2):
@@ -249,9 +253,9 @@
         for r in range(1, Y):
             for group in range(X):
                 part_y(r, group).wait_recv()
-        total = y_send[y]
+        total = fg_part[:, core, y] + c_recv[:, y]
         for r in range(1, Y):
-            total = total + y_recv[r - 1]
+            total = total + y_recv[r - 1].astype(F32)
         x_send[...] = total
         for r in range(1, X):
             part_x(r).start()
@@ -284,18 +288,10 @@
             if step < HALF:
                 pl.when(j == step)(event)
 
-    early = ((1, relay_x), (3, relay_y), (6, relay_c))
+    early = ((2, relay_x), (5, relay_y), (HALF, relay_c))
     late = ((2, sum_y), (4, sum_x), (6, sum_z))
 
     def first_half(j, carry):
-        @pl.when(j + lay.ahead < HALF)
-        def _():
-            produce(j + lay.ahead)
-
-        @pl.when(j + lay.ahead < NC)
-        def _():
-            send(j + lay.ahead)
-
         scheduled(j, early)
         a, b = j, j + HALF
         ga = forward(e_own[...], g[a])
@@ -306,13 +302,13 @@
         halo_p(a).wait_recv()
         pa = pa + forward(e_prev[...], p_prev[a])
         pa_hat[j] = pa
-        fg_part[a] = inverse(inv_tab[0], *correlate(pa, ga)).reshape(2, FL // 2, CH)
+        fg_part[a] = inverse(inv_tab[0], *correlate(pa, ga)).reshape(2, Y, lay.rows, CH)
         pair(a).start()
         gb = forward(e_own[...], g[b])
         halo_g(b).wait_recv()
         gb = gb + forward(e_next[...], g_next[b])
         gb_hat[j] = gb
-        fg_part[b] = inverse(inv_tab[0], *correlate(pb, gb)).reshape(2, FL // 2, CH)
+        fg_part[b] = inverse(inv_tab[0], *correlate(pb, gb)).reshape(2, Y, lay.rows, CH)
         pair(b).start()
 
         @pl.when(j > 0)
@@ -341,35 +337,23 @@
             [tap_all[:, n * per + i].reshape(FL, lay.lanes) for i in range(per)], 1
         )
 
-    def rounded(value):
-        return (value * (1.0 / BINS)).astype(BF16).astype(F32)
-
-    def write_query(n, mixed):
+    def write(ref, n, value):
         cols = pl.ds(pl.multiple_of(n * CH, CH), CH)
-        qg_ref[:, cols] = (o[n].astype(F32) * mixed).astype(BF16)
-
-    def write_kv(n, back):
-        cols = pl.ds(pl.multiple_of(n * CH, CH), CH)
-        kg_ref[:, cols] = (back * v[n].astype(F32)).astype(BF16)
-        vg_ref[:, cols] = (back * k[n].astype(F32)).astype(BF16)
+        ref[:, cols] = (value * (1.0 / BINS)).astype(BF16)
 
     def second_half(j, carry):
-        @pl.when(j + HALF + lay.ahead < NC)
-        def _():
-            send(j + HALF + lay.ahead)
-
         scheduled(j, late)
         a, b = j, j + HALF
         ha = forward(fwd_tab[0], taps_of(a))
-        write_query(a, rounded(inverse(d_own[...], *convolve(ha, pa_hat[j]))))
+        write(mixed_ref, a, inverse(d_own[...], *convolve(ha, pa_hat[j])))
         hb = forward(fwd_tab[0], taps_of(b))
-        write_kv(b, rounded(inverse(d_own[...], *correlate(hb, gb_hat[j]))))
+        write(back_ref, b, inverse(d_own[...], *correlate(hb, gb_hat[j])))
         halo_g(a).wait_recv()
         ga = ga_hat[j] + forward(e_next[...], g_next[a])
-        write_kv(a, rounded(inverse(d_own[...], *correlate(ha, ga))))
+        write(back_ref, a, inverse(d_own[...], *correlate(ha, ga)))
         halo_p(b).wait_recv()
         pb = pb_hat[j] + forward(e_prev[...], p_prev[b])
-        write_query(b, rounded(inverse(d_own[...], *convolve(hb, pb))))
+        write(mixed_ref, b, inverse(d_own[...], *convolve(hb, pb)))
         return carry
 
     lax.fori_loop(0, HALF, second_half, 0)
@@ -378,7 +362,7 @@
             event()
     for r in range(1, DP):
         part_f(r).wait_recv()
-    fg_ref[...] = final[...].reshape(FL, lay.lanes).T * (scale / BINS)
+    fg_ref[...] = final[...].reshape(FL, lay.lanes).T
 
     def drain(n, carry):
         halo_p(n).wait_send()
@@ -416,20 +400,20 @@
     spectra = pltpu.VMEM((lay.half, N, CH), F32)
     mat = pltpu.VMEM((N, 2 * FL), BF16)
     dma = pltpu.SemaphoreType.DMA
-    return pl.pallas_call(
-        functools.partial(kernel, lay, scale),
+    mixed, back, filter_grad = pl.pallas_call(
+        functools.partial(kernel, lay),
         in_specs=[any_spec] * 4 + [vmem] * 4,
-        out_specs=[vmem] * 4,
-        out_shape=[acts, acts, acts, jax.ShapeDtypeStruct(filter_taps.shape, F32)],
+        out_specs=[vmem] * 3,
+        out_shape=[acts, acts, jax.ShapeDtypeStruct(filter_taps.shape, F32)],
         scratch_shapes=[block] * 8 + [spectra] * 4 + [
             mat, mat, mat,
             pltpu.VMEM((2 * FL, 2 * N), BF16),
             pltpu.VMEM((DP, lay.rows, lay.lanes), BF16),
             pltpu.VMEM((DP, lay.ctx, lay.rows, lay.lanes), BF16),
-            pltpu.VMEM((NC, 2, FL // 2, CH), F32),
-            pltpu.VMEM((NC, FL // 2, CH), F32),
-            pltpu.VMEM((Y, NC, lay.rows, CH), F32),
-            pltpu.VMEM((Y - 1, NC, lay.rows, CH), F32),
+            pltpu.VMEM((NC, 2, Y, lay.rows, CH), F32),
+            pltpu.VMEM((NC, Y, lay.rows, CH), F32),
+            pltpu.VMEM((Y, NC, lay.rows, CH), BF16),
+            pltpu.VMEM((Y - 1, NC, lay.rows, CH), BF16),
             pltpu.VMEM((NC, lay.rows, CH), F32),
             pltpu.VMEM((X - 1, GC, lay.rows, CH), F32),
             pltpu.VMEM((Z, lay.rows, lay.lanes), F32),
@@ -447,6 +431,11 @@
         name="mixer",
     )(query_act, key_act, value_act, out_grad, filter_taps,
       doc_ids.reshape(-1, FL), jnp.asarray(fwd_tab), jnp.asarray(inv_tab))
+    mixed, back = mixed.astype(F32), back.astype(F32)
+    query_grad = (out_grad.astype(F32) * mixed).astype(BF16)
+    key_grad = (back * value_act.astype(F32)).astype(BF16)
+    value_grad = (back * key_act.astype(F32)).astype(BF16)
+    return query_grad, key_grad, value_grad, filter_grad * (scale / BINS)
 
 
 def solution(mesh):

time: 74.8 us -> 76.3 us (1.020)
  the two profiles are of different devices: /device:TPU:5 before, /device:TPU:1 now
where the time goes in v3:
time: 76.3 us; the launch traced here: 76.1 us
  Pallas kernels  70 us (92%)
  other arithmetic  5.47 us (7%)
    pallas_call x1, Pallas kernels, shards(): pl.pallas_call(functools.partial(kernel, lay), in_specs=[any_spec] * 4 +...  70 us
    convert_element_type x1, other arithmetic, shards(): value_grad = (back * key_act.astype(F32)).astype(BF16)  3.99 us

profile of v3, /device:TPU:1, one launch (start us, length us, event | category | flops | bytes accessed | tf_op | source)
XLA Modules:
  0.0 76.1 jit_solution(12444461446230671455)
XLA Ops:
  0.6 0.0 copy-start
  0.6 0.0 copy-start.1
  0.7 0.0 copy-start.2
  0.7 70.0 %mixer.1 = (bf16[128,4096]{1,0:T(8,128)(2,1)}, bf16[128,4096]{1,0:T(8,128)(2,1)}, f32[128,128]{1,0:T(8,128)}) custom-call(bf16[128,4096]{1,0:T(8,128)(2,1)} %q_hbm.1, bf16[128,4096]{1,0:T(8,128)(2,1)} %k_hbm.1, bf16[128,4096]{1,0:T(8,128)(2,1)} %v_hbm.1, bf16[128,4096]{1,0:T(8,128)(2,1)} %o_hbm.1, f32[128,128]{1,0:T(8,128)} %taps.1, s32[256,128]{1,0:T(8,128)} %bitcast.1, ...), custom_call_target="tpu_custom_call" | custom-call | tf_op jit(solution)/shard_map/mixer/pallas_call | solution.py:403
  70.6 1.5 %broadcast_multiply_fusion = f32[128,128]{1,0:T(8,128)} fusion(f32[128,128]{1,0:T(8,128)} %get-tuple-element.9), kind=kLoop, calls=%fused_computation.5 | loop fusion | flops 16384 | bytes 131072 | tf_op jit(solution)/shard_map/mul | solution.py:438
  72.1 0.0 copy-done
  72.1 0.0 copy-done.1
  72.1 0.0 copy-done.2
  72.1 4.0 %fusion.1 = (bf16[128,4096]{1,0:T(8,128)(2,1)}, bf16[128,4096]{1,0:T(8,128)(2,1)}, bf16[128,4096]{1,0:T(8,128)(2,1)}) fusion(bf16[128,4096]{1,0:T(8,128)(2,1)} %get-tuple-element.8, bf16[128,4096]{1,0:T(8,128)(2,1)S(1)} %copy-done, bf16[128,4096]{1,0:T(8,128)(2,1)S(1)} %copy-done.1, bf16[128,4096]{1,0:T(8,128)(2,1)} %get-tuple-element.7, ...), kind=kLoop, calls=%fused_computation.3 | loop fusion | flops 5767168 | bytes 8388608 | tf_op jit(solution)/shard_map/convert_element_type | solution.py:437
Async XLA Ops:
  0.6 71.5 %copy-start = (bf16[128,4096]{1,0:T(8,128)(2,1)S(1)}, bf16[128,4096]{1,0:T(8,128)(2,1)}, u32[]{:S(2)}) copy-start(bf16[128,4096]{1,0:T(8,128)(2,1)} %k_hbm.1) | copy-start | bytes 3145732
  0.6 71.5 %copy-start.1 = (bf16[128,4096]{1,0:T(8,128)(2,1)S(1)}, bf16[128,4096]{1,0:T(8,128)(2,1)}, u32[]{:S(2)}) copy-start(bf16[128,4096]{1,0:T(8,128)(2,1)} %v_hbm.1) | copy-start | bytes 3145732
  0.7 71.5 %copy-start.2 = (bf16[128,4096]{1,0:T(8,128)(2,1)S(1)}, bf16[128,4096]{1,0:T(8,128)(2,1)}, u32[]{:S(2)}) copy-start(bf16[128,4096]{1,0:T(8,128)(2,1)} %o_hbm.1) | copy-start | bytes 3145732

commit v4 on v3

--- a/solution.py
+++ b/solution.py
@@ -66,12 +66,10 @@
 class Layout:
     def __init__(self, dp, ctx, chans, chunk=CHUNK):
         self.dp, self.ctx, self.cores, self.ys = dp, ctx, 2, dp // 2
-        self.zs = 8 if ctx == 32 else ctx // 2
-        self.xs = ctx // self.zs
         self.chans, self.chunk = chans, chunk
         self.chunks = chans // chunk
         self.half = self.chunks // 2
-        self.group = self.chunks // self.xs
+        self.batch = max(1, self.half // 4)
         self.rows = FL // dp
         self.lanes = chans // ctx
 
@@ -83,35 +81,38 @@
     )
 
 
-def kernel(lay, q_hbm, k_hbm, v_hbm, o_hbm, taps, docs, fwd_tab, inv_tab,
+def kernel(lay, scale, q_hbm, k_hbm, v_hbm, o_hbm, taps, docs, fwd_tab, inv_tab,
            mixed_ref, back_ref, fg_ref,
            q, k, v, o, p, g, p_prev, g_next, pa_hat, ga_hat, pb_hat, gb_hat,
            e_own, e_prev, e_next, d_own, tap_own, tap_all, fg_part, c_recv, y_send, y_recv,
-           x_send, x_recv, z_send, z_recv, final,
-           in_sem, p_ssem, p_rsem, g_ssem, g_rsem, tz_ssem, tz_rsem, tx_ssem, tx_rsem,
+           x_own, x_send, x_recv, final,
+           in_sem, p_ssem, p_rsem, g_ssem, g_rsem, tx_ssem, tx_rsem,
            ty_ssem, ty_rsem, tc_ssem, tc_rsem, c_ssem, c_rsem, y_ssem, y_rsem,
-           x_ssem, x_rsem, z_ssem, z_rsem, f_ssem, f_rsem):
+           x_ssem, x_rsem, f_ssem, f_rsem):
     dp, ctx = lax.axis_index("dp"), lax.axis_index("ctx")
-    DP, CTX, X, Y, Z = lay.dp, lay.ctx, lay.xs, lay.ys, lay.zs
-    NC, HALF, GC, CH = lay.chunks, lay.half, lay.group, lay.chunk
+    DP, CTX, Y = lay.dp, lay.ctx, lay.ys
+    NC, HALF, YB, CH = lay.chunks, lay.half, lay.batch, lay.chunk
     y, core = lax.div(dp, 2), lax.rem(dp, 2)
-    x, z = lax.div(ctx, Z), lax.rem(ctx, Z)
     me = dp * CTX + ctx
     after, before = lax.rem(me + 1, DP * CTX), lax.rem(me + DP * CTX - 1, DP * CTX)
     place = lambda flat: (lax.div(flat, CTX), lax.rem(flat, CTX))
     nxt, prv = place(after), place(before)
-    z_peer = lambda r: (dp, x * Z + lax.rem(z + r, Z))
-    x_peer = lambda r: (dp, lax.rem(x + r, X) * Z + z)
+    c_peer = lambda r: (dp, lax.rem(ctx + r, CTX))
     y_peer = lambda r: (2 * lax.rem(y + r, Y) + core, ctx)
     d_peer = lambda r: (lax.rem(dp + r, DP), ctx)
     partner = (2 * y + 1 - core, ctx)
     slot = core * Y + y
 
     barrier = pltpu.get_barrier_semaphore()
-    peers = [nxt, prv] + [z_peer(r) for r in range(1, Z)]
-    peers += [x_peer(r) for r in range(1, X)] + [d_peer(r) for r in range(1, DP)]
+    peers = [nxt, prv] + [d_peer(r) for r in range(1, DP)]
     for peer in peers:
         pl.semaphore_signal(barrier, inc=1, device_id=peer, device_id_type=MESH)
+
+    def greet(r, carry):
+        pl.semaphore_signal(barrier, inc=1, device_id=c_peer(r), device_id_type=MESH)
+        return carry
+
+    lax.fori_loop(1, CTX, greet, 0)
 
     def load(which, n):
         hbm, ref = ((q_hbm, q), (k_hbm, k), (v_hbm, v), (o_hbm, o))[which]
@@ -151,13 +152,9 @@
         d0, d1 = inv_tab[0, rows, :].astype(F32), inv_tab[1, rows, :].astype(F32)
         d_own[rows, :] = (d0 * (1.0 - wide) + d1 * wide).astype(BF16)
 
-    def tap_z(r):
+    def tap_ctx(r):
         here = tap_all.at[slot, ctx]
-        return remote(here, here, tz_ssem.at[r - 1], tz_rsem.at[r - 1], z_peer(r))
-
-    def tap_x(r):
-        here = tap_all.at[slot, pl.ds(x * Z, Z)]
-        return remote(here, here, tx_ssem.at[r - 1], tx_rsem.at[r - 1], x_peer(r))
+        return remote(here, here, tx_ssem.at[r - 1], tx_rsem.at[r - 1], c_peer(r))
 
     def tap_y(r):
         here = tap_all.at[slot]
@@ -177,17 +174,20 @@
         return remote(fg_part.at[n, 1 - core], c_recv.at[n], c_ssem.at[n], c_rsem.at[n], partner)
 
     def part_y(r, group):
-        chunks = pl.ds(group * GC, GC)
+        chunks = pl.ds(group * YB, YB)
         return remote(y_send.at[lax.rem(y + r, Y), chunks], y_recv.at[r - 1, chunks],
                       y_ssem.at[r - 1, group], y_rsem.at[r - 1, group], y_peer(r))
 
-    def part_x(r):
-        return remote(x_send.at[pl.ds(lax.rem(x + r, X) * GC, GC)], x_recv.at[r - 1],
-                      x_ssem.at[r - 1], x_rsem.at[r - 1], x_peer(r))
-
-    def part_z(r):
-        return remote(z_send.at[lax.rem(z + r, Z)], z_recv.at[r - 1],
-                      z_ssem.at[r - 1], z_rsem.at[r - 1], z_peer(r))
+    def part_ctx(r):
+        return remote(x_send.at[lax.rem(ctx + r, CTX)], x_recv.at[r - 1],
+                      x_ssem.at[r - 1], x_rsem.at[r - 1], c_peer(r))
+
+    def each_peer(action):
+        def body(r, carry):
+            action(r)
+            return carry
+
+        lax.fori_loop(1, CTX, body, 0)
 
     def part_f(r):
         here = final.at[slot]
@@ -216,9 +216,8 @@
         return carry
 
     produce(0)
-    pl.semaphore_wait(barrier, len(peers))
-    for r in range(1, Z):
-        tap_z(r).start()
+    pl.semaphore_wait(barrier, len(peers) + CTX - 1)
+    each_peer(lambda r: tap_ctx(r).start())
     send(0)
     lax.fori_loop(1, HALF, produce_and_send, 0)
     lax.fori_loop(HALF, NC, send_rest, 0)
@@ -228,19 +227,12 @@
         y_send[:, n] = (fg_part[n, core] + c_recv[n]).astype(BF16)
 
     def send_groups(gi):
-        for group in (gi, gi + X // 2):
+        for group in (gi, gi + HALF // YB):
             for r in range(1, Y):
                 part_y(r, group).start()
 
-    def relay_x():
-        for r in range(1, Z):
-            tap_z(r).wait_recv()
-        for r in range(1, X):
-            tap_x(r).start()
-
     def relay_y():
-        for r in range(1, X):
-            tap_x(r).wait_recv()
+        each_peer(lambda r: tap_ctx(r).wait_recv())
         for r in range(1, Y):
             tap_y(r).start()
 
@@ -251,35 +243,22 @@
 
     def sum_y():
         for r in range(1, Y):
-            for group in range(X):
+            for group in range(NC // YB):
                 part_y(r, group).wait_recv()
         total = fg_part[:, core, y] + c_recv[:, y]
         for r in range(1, Y):
             total = total + y_recv[r - 1].astype(F32)
-        x_send[...] = total
-        for r in range(1, X):
-            part_x(r).start()
-
-    def sum_x():
-        for r in range(1, X):
-            part_x(r).wait_recv()
-        total = x_send[pl.ds(x * GC, GC)]
-        for r in range(1, X):
-            total = total + x_recv[r - 1]
         per = CH // lay.lanes
-        for i in range(Z):
+        for i in range(CTX):
             lane = (i % per) * lay.lanes
-            z_send[i] = total[i // per, :, lane : lane + lay.lanes]
-        for r in range(1, Z):
-            part_z(r).start()
-
-    def sum_z():
-        for r in range(1, Z):
-            part_z(r).wait_recv()
-        total = z_send[z]
-        for r in range(1, Z):
-            total = total + z_recv[r - 1]
-        final[slot] = total
+            piece = total[i // per, :, lane : lane + lay.lanes]
+            x_own[i] = piece
+            x_send[i] = piece.astype(BF16)
+        each_peer(lambda r: part_ctx(r).start())
+
+    def sum_ctx():
+        each_peer(lambda r: part_ctx(r).wait_recv())
+        final[slot] = x_own[ctx] + jnp.sum(x_recv[...].astype(F32), axis=0)
         for r in range(1, DP):
             part_f(r).start()
 
@@ -288,8 +267,8 @@
             if step < HALF:
                 pl.when(j == step)(event)
 
-    early = ((2, relay_x), (5, relay_y), (HALF, relay_c))
-    late = ((2, sum_y), (4, sum_x), (6, sum_z))
+    early = ((4, relay_y), (HALF, relay_c))
+    late = ((4, sum_y), (HALF, sum_ctx))
 
     def first_half(j, carry):
         scheduled(j, early)
@@ -316,9 +295,9 @@
             absorb(j - 1)
             absorb(j - 1 + HALF)
 
-        @pl.when((j > 0) & (lax.rem(j, GC) == 0))
+        @pl.when((j > 0) & (lax.rem(j, YB) == 0))
         def _():
-            send_groups(lax.div(j, GC) - 1)
+            send_groups(lax.div(j, YB) - 1)
 
         return carry
 
@@ -328,7 +307,7 @@
             event()
     absorb(HALF - 1)
     absorb(NC - 1)
-    send_groups(HALF // GC - 1)
+    send_groups(HALF // YB - 1)
     tap_c().wait_recv()
 
     def taps_of(n):
@@ -362,7 +341,7 @@
             event()
     for r in range(1, DP):
         part_f(r).wait_recv()
-    fg_ref[...] = final[...].reshape(FL, lay.lanes).T
+    fg_ref[...] = final[...].reshape(FL, lay.lanes).T * (scale / BINS)
 
     def drain(n, carry):
         halo_p(n).wait_send()
@@ -371,15 +350,11 @@
         return carry
 
     lax.fori_loop(0, NC, drain, 0)
-    for r in range(1, Z):
-        tap_z(r).wait_send()
-        part_z(r).wait_send()
-    for r in range(1, X):
-        tap_x(r).wait_send()
-        part_x(r).wait_send()
+    each_peer(lambda r: tap_ctx(r).wait_send())
+    each_peer(lambda r: part_ctx(r).wait_send())
     for r in range(1, Y):
         tap_y(r).wait_send()
-        for group in range(X):
+        for group in range(NC // YB):
             part_y(r, group).wait_send()
     for r in range(1, DP):
         part_f(r).wait_send()
@@ -393,15 +368,13 @@
     fwd_tab, inv_tab = tables()
     acts = jax.ShapeDtypeStruct((rows, chans), BF16)
     any_spec, vmem = pl.BlockSpec(memory_space=pl.ANY), pl.BlockSpec(memory_space=pltpu.VMEM)
-    NC, CH, GC, DP, X, Y, Z = (
-        lay.chunks, lay.chunk, lay.group, lay.dp, lay.xs, lay.ys, lay.zs
-    )
+    NC, CH, CTX, DP, Y = lay.chunks, lay.chunk, lay.ctx, lay.dp, lay.ys
     block = pltpu.VMEM((NC, FL, CH), BF16)
     spectra = pltpu.VMEM((lay.half, N, CH), F32)
     mat = pltpu.VMEM((N, 2 * FL), BF16)
     dma = pltpu.SemaphoreType.DMA
     mixed, back, filter_grad = pl.pallas_call(
-        functools.partial(kernel, lay),
+        functools.partial(kernel, lay, scale),
         in_specs=[any_spec] * 4 + [vmem] * 4,
         out_specs=[vmem] * 3,
         out_shape=[acts, acts, jax.ShapeDtypeStruct(filter_taps.shape, F32)],
@@ -409,21 +382,19 @@
             mat, mat, mat,
             pltpu.VMEM((2 * FL, 2 * N), BF16),
             pltpu.VMEM((DP, lay.rows, lay.lanes), BF16),
-            pltpu.VMEM((DP, lay.ctx, lay.rows, lay.lanes), BF16),
+            pltpu.VMEM((DP, CTX, lay.rows, lay.lanes), BF16),
             pltpu.VMEM((NC, 2, Y, lay.rows, CH), F32),
             pltpu.VMEM((NC, Y, lay.rows, CH), F32),
             pltpu.VMEM((Y, NC, lay.rows, CH), BF16),
             pltpu.VMEM((Y - 1, NC, lay.rows, CH), BF16),
-            pltpu.VMEM((NC, lay.rows, CH), F32),
-            pltpu.VMEM((X - 1, GC, lay.rows, CH), F32),
-            pltpu.VMEM((Z, lay.rows, lay.lanes), F32),
-            pltpu.VMEM((Z - 1, lay.rows, lay.lanes), F32),
+            pltpu.VMEM((CTX, lay.rows, lay.lanes), F32),
+            pltpu.VMEM((CTX, lay.rows, lay.lanes), BF16),
+            pltpu.VMEM((CTX - 1, lay.rows, lay.lanes), BF16),
             pltpu.VMEM((DP, lay.rows, lay.lanes), F32),
             dma((4, NC)), dma((NC,)), dma((NC,)), dma((NC,)), dma((NC,)),
-            dma((Z - 1,)), dma((Z - 1,)), dma((X - 1,)), dma((X - 1,)),
-            dma((Y - 1,)), dma((Y - 1,)), dma, dma, dma((NC,)), dma((NC,)),
-            dma((Y - 1, X)), dma((Y - 1, X)), dma((X - 1,)), dma((X - 1,)),
-            dma((Z - 1,)), dma((Z - 1,)), dma((DP - 1,)), dma((DP - 1,)),
+            dma((CTX - 1,)), dma((CTX - 1,)), dma((Y - 1,)), dma((Y - 1,)), dma, dma,
+            dma((NC,)), dma((NC,)), dma((Y - 1, NC // lay.batch)), dma((Y - 1, NC // lay.batch)),
+            dma((CTX - 1,)), dma((CTX - 1,)), dma((DP - 1,)), dma((DP - 1,)),
         ],
         compiler_params=pltpu.CompilerParams(
             collective_id=0, has_side_effects=True, vmem_limit_bytes=60 * 2**20
@@ -435,7 +406,7 @@
     query_grad = (out_grad.astype(F32) * mixed).astype(BF16)
     key_grad = (back * value_act.astype(F32)).astype(BF16)
     value_grad = (back * key_act.astype(F32)).astype(BF16)
-    return query_grad, key_grad, value_grad, filter_grad * (scale / BINS)
+    return query_grad, key_grad, value_grad, filter_grad
 
 
 def solution(mesh):

time: 76.3 us -> 73.1 us (0.958)
  Pallas kernels: 70 us -> 67.6 us
  other arithmetic: 5.47 us -> 4.03 us
    pallas_call x1, Pallas kernels: 70 us -> 67.6 us  [shards(): pl.pallas_call(functools.partial(kernel, lay, scale), in_specs=[any_spec]...]
    mul x1 -> x0, other arithmetic: 1.48 us -> none  [shards(): return (query_grad, key_grad, value_grad, filter_grad * (scale / BINS))]
where the time goes in v4:
time: 73.1 us; the launch traced here: 73 us
  Pallas kernels  67.6 us (92%)
  other arithmetic  4.03 us (6%)
    pallas_call x1, Pallas kernels, shards(): pl.pallas_call(functools.partial(kernel, lay, scale), in_specs=[any_spec]...  67.6 us
    convert_element_type x1, other arithmetic, shards(): value_grad = (back * key_act.astype(F32)).astype(BF16)  4.03 us

profile of v4, /device:TPU:1, one launch (start us, length us, event | category | flops | bytes accessed | tf_op | source)
XLA Modules:
  0.0 73.0 jit_solution(5878416128778135802)
XLA Ops:
  0.6 0.0 copy-start
  0.6 0.0 copy-start.1
  0.7 0.0 copy-start.2
  0.7 67.6 %mixer.1 = (bf16[128,4096]{1,0:T(8,128)(2,1)}, bf16[128,4096]{1,0:T(8,128)(2,1)}, f32[128,128]{1,0:T(8,128)}) custom-call(bf16[128,4096]{1,0:T(8,128)(2,1)} %q_hbm.1, bf16[128,4096]{1,0:T(8,128)(2,1)} %k_hbm.1, bf16[128,4096]{1,0:T(8,128)(2,1)} %v_hbm.1, bf16[128,4096]{1,0:T(8,128)(2,1)} %o_hbm.1, f32[128,128]{1,0:T(8,128)} %taps.1, s32[256,128]{1,0:T(8,128)} %bitcast.1, ...), custom_call_target="tpu_custom_call" | custom-call | tf_op jit(solution)/shard_map/mixer/pallas_call | solution.py:376
  68.3 0.0 copy-done
  68.3 0.0 copy-done.1
  68.3 0.0 copy-done.2
  68.3 0.0 copy-start.3
  68.3 4.0 %fusion.1 = (bf16[128,4096]{1,0:T(8,128)(2,1)}, bf16[128,4096]{1,0:T(8,128)(2,1)}, bf16[128,4096]{1,0:T(8,128)(2,1)}) fusion(bf16[128,4096]{1,0:T(8,128)(2,1)} %get-tuple-element.8, bf16[128,4096]{1,0:T(8,128)(2,1)S(1)} %copy-done, bf16[128,4096]{1,0:T(8,128)(2,1)S(1)} %copy-done.1, bf16[128,4096]{1,0:T(8,128)(2,1)} %get-tuple-element.7, ...), kind=kLoop, calls=%fused_computation.3 | loop fusion | flops 5767168 | bytes 8388608 | tf_op jit(solution)/shard_map/convert_element_type | solution.py:408
  72.3 0.0 copy-done.3
  72.3 0.6 copy.13
Async XLA Ops:
  0.6 67.6 %copy-start = (bf16[128,4096]{1,0:T(8,128)(2,1)S(1)}, bf16[128,4096]{1,0:T(8,128)(2,1)}, u32[]{:S(2)}) copy-start(bf16[128,4096]{1,0:T(8,128)(2,1)} %k_hbm.1) | copy-start | bytes 3145732
  0.6 67.6 %copy-start.1 = (bf16[128,4096]{1,0:T(8,128)(2,1)S(1)}, bf16[128,4096]{1,0:T(8,128)(2,1)}, u32[]{:S(2)}) copy-start(bf16[128,4096]{1,0:T(8,128)(2,1)} %v_hbm.1) | copy-start | bytes 3145732
  0.7 67.6 %copy-start.2 = (bf16[128,4096]{1,0:T(8,128)(2,1)S(1)}, bf16[128,4096]{1,0:T(8,128)(2,1)}, u32[]{:S(2)}) copy-start(bf16[128,4096]{1,0:T(8,128)(2,1)} %o_hbm.1) | copy-start | bytes 3145732
  68.3 4.0 %copy-start.3 = (f32[128,128]{1,0:T(8,128)S(1)}, f32[128,128]{1,0:T(8,128)}, u32[]{:S(2)}) copy-start(f32[128,128]{1,0:T(8,128)} %get-tuple-element.20) | copy-start | bytes 196612

commit v5 on v4

--- a/solution.py
+++ b/solution.py
@@ -28,12 +28,7 @@
         high = full.astype(ml_dtypes.bfloat16)
         low = (full - high.astype(np.float64)).astype(ml_dtypes.bfloat16)
         fwd.append(np.concatenate([high, low], 1))
-        zero = np.zeros_like(low.T)
-        inv.append(
-            np.concatenate(
-                [np.concatenate([high.T, high.T], 1), np.concatenate([low.T, zero], 1)], 0
-            )
-        )
+        inv.append(np.concatenate([high.T, low.T], 0))
     return np.stack(fwd), np.stack(inv[:2])
 
 
@@ -44,10 +39,8 @@
 
 
 def inverse(matrix, cosines, sines):
-    spectrum = jnp.concatenate([cosines, sines], 0)
-    high = spectrum.astype(BF16)
-    low = (spectrum - high.astype(F32)).astype(BF16)
-    both = jnp.dot(matrix, jnp.concatenate([high, low], 0), preferred_element_type=F32)
+    spectrum = jnp.concatenate([cosines, sines], 0).astype(BF16)
+    both = jnp.dot(matrix, spectrum, preferred_element_type=F32)
     return both[:FL] + both[FL:]
 
 
@@ -83,10 +76,10 @@
 
 def kernel(lay, scale, q_hbm, k_hbm, v_hbm, o_hbm, taps, docs, fwd_tab, inv_tab,
            mixed_ref, back_ref, fg_ref,
-           q, k, v, o, p, g, p_prev, g_next, pa_hat, ga_hat, pb_hat, gb_hat,
+           q, k, v, o, p, g, p_prev, g_next, mixed, back, pa_hat, ga_hat, pb_hat, gb_hat,
            e_own, e_prev, e_next, d_own, tap_own, tap_all, fg_part, c_recv, y_send, y_recv,
            x_own, x_send, x_recv, final,
-           in_sem, p_ssem, p_rsem, g_ssem, g_rsem, tx_ssem, tx_rsem,
+           in_sem, out_sem, p_ssem, p_rsem, g_ssem, g_rsem, tx_ssem, tx_rsem,
            ty_ssem, ty_rsem, tc_ssem, tc_rsem, c_ssem, c_rsem, y_ssem, y_rsem,
            x_ssem, x_rsem, f_ssem, f_rsem):
     dp, ctx = lax.axis_index("dp"), lax.axis_index("ctx")
@@ -146,7 +139,7 @@
     e_prev[...] = (-t2 * twice(keep_prev)).astype(BF16)
     e_next[...] = ((t1 * (1.0 - split) + t2 * split) * twice(keep_next)).astype(BF16)
     square = jnp.broadcast_to(moved, (FL, FL)).T
-    wide = jnp.concatenate([square] * (2 * N // FL), 1)
+    wide = jnp.concatenate([square] * (N // FL), 1)
     for half in range(2):
         rows = pl.ds(half * FL, FL)
         d0, d1 = inv_tab[0, rows, :].astype(F32), inv_tab[1, rows, :].astype(F32)
@@ -267,27 +260,25 @@
             if step < HALF:
                 pl.when(j == step)(event)
 
-    early = ((4, relay_y), (HALF, relay_c))
+    early = ((0, relay_y), (min(5, HALF - 1), relay_c))
     late = ((4, sum_y), (HALF, sum_ctx))
 
     def first_half(j, carry):
         scheduled(j, early)
         a, b = j, j + HALF
+        halo_p(a).wait_recv()
+        halo_g(b).wait_recv()
         ga = forward(e_own[...], g[a])
         pb = forward(e_own[...], p[b])
+        pa = forward(e_own[...], p[a]) + forward(e_prev[...], p_prev[a])
+        gb = forward(e_own[...], g[b]) + forward(e_next[...], g_next[b])
         ga_hat[j] = ga
         pb_hat[j] = pb
-        pa = forward(e_own[...], p[a])
-        halo_p(a).wait_recv()
-        pa = pa + forward(e_prev[...], p_prev[a])
         pa_hat[j] = pa
+        gb_hat[j] = gb
         fg_part[a] = inverse(inv_tab[0], *correlate(pa, ga)).reshape(2, Y, lay.rows, CH)
+        fg_part[b] = inverse(inv_tab[0], *correlate(pb, gb)).reshape(2, Y, lay.rows, CH)
         pair(a).start()
-        gb = forward(e_own[...], g[b])
-        halo_g(b).wait_recv()
-        gb = gb + forward(e_next[...], g_next[b])
-        gb_hat[j] = gb
-        fg_part[b] = inverse(inv_tab[0], *correlate(pb, gb)).reshape(2, Y, lay.rows, CH)
         pair(b).start()
 
         @pl.when(j > 0)
@@ -302,9 +293,6 @@
         return carry
 
     lax.fori_loop(0, HALF, first_half, 0)
-    for step, event in early:
-        if step >= HALF:
-            event()
     absorb(HALF - 1)
     absorb(NC - 1)
     send_groups(HALF // YB - 1)
@@ -317,22 +305,30 @@
         )
 
     def write(ref, n, value):
-        cols = pl.ds(pl.multiple_of(n * CH, CH), CH)
-        ref[:, cols] = (value * (1.0 / BINS)).astype(BF16)
+        ref[n] = (value * (1.0 / BINS)).astype(BF16)
+
+    def store(which, n):
+        ref, hbm = ((mixed, mixed_ref), (back, back_ref))[which]
+        return pltpu.make_async_copy(
+            ref.at[n], hbm.at[:, pl.ds(pl.multiple_of(n * CH, CH), CH)], out_sem.at[which, n]
+        )
 
     def second_half(j, carry):
         scheduled(j, late)
         a, b = j, j + HALF
+        halo_g(a).wait_recv()
+        halo_p(b).wait_recv()
         ha = forward(fwd_tab[0], taps_of(a))
-        write(mixed_ref, a, inverse(d_own[...], *convolve(ha, pa_hat[j])))
         hb = forward(fwd_tab[0], taps_of(b))
-        write(back_ref, b, inverse(d_own[...], *correlate(hb, gb_hat[j])))
-        halo_g(a).wait_recv()
         ga = ga_hat[j] + forward(e_next[...], g_next[a])
-        write(back_ref, a, inverse(d_own[...], *correlate(ha, ga)))
-        halo_p(b).wait_recv()
         pb = pb_hat[j] + forward(e_prev[...], p_prev[b])
-        write(mixed_ref, b, inverse(d_own[...], *convolve(hb, pb)))
+        write(mixed, a, inverse(d_own[...], *convolve(ha, pa_hat[j])))
+        write(back, a, inverse(d_own[...], *correlate(ha, ga)))
+        write(mixed, b, inverse(d_own[...], *convolve(hb, pb)))
+        write(back, b, inverse(d_own[...], *correlate(hb, gb_hat[j])))
+        for n in (a, b):
+            store(0, n).start()
+            store(1, n).start()
         return carry
 
     lax.fori_loop(0, HALF, second_half, 0)
@@ -347,6 +343,8 @@
         halo_p(n).wait_send()
         halo_g(n).wait_send()
         pair(n).wait_send()
+        store(0, n).wait()
+        store(1, n).wait()
         return carry
 
     lax.fori_loop(0, NC, drain, 0)
@@ -376,11 +374,11 @@
     mixed, back, filter_grad = pl.pallas_call(
         functools.partial(kernel, lay, scale),
         in_specs=[any_spec] * 4 + [vmem] * 4,
-        out_specs=[vmem] * 3,
+        out_specs=[any_spec, any_spec, vmem],
         out_shape=[acts, acts, jax.ShapeDtypeStruct(filter_taps.shape, F32)],
-        scratch_shapes=[block] * 8 + [spectra] * 4 + [
+        scratch_shapes=[block] * 10 + [spectra] * 4 + [
             mat, mat, mat,
-            pltpu.VMEM((2 * FL, 2 * N), BF16),
+            pltpu.VMEM((2 * FL, N), BF16),
             pltpu.VMEM((DP, lay.rows, lay.lanes), BF16),
             pltpu.VMEM((DP, CTX, lay.rows, lay.lanes), BF16),
             pltpu.VMEM((NC, 2, Y, lay.rows, CH), F32),
@@ -391,13 +389,13 @@
             pltpu.VMEM((CTX, lay.rows, lay.lanes), BF16),
             pltpu.VMEM((CTX - 1, lay.rows, lay.lanes), BF16),
             pltpu.VMEM((DP, lay.rows, lay.lanes), F32),
-            dma((4, NC)), dma((NC,)), dma((NC,)), dma((NC,)), dma((NC,)),
+            dma((4, NC)), dma((2, NC)), dma((NC,)), dma((NC,)), dma((NC,)), dma((NC,)),
             dma((CTX - 1,)), dma((CTX - 1,)), dma((Y - 1,)), dma((Y - 1,)), dma, dma,
             dma((NC,)), dma((NC,)), dma((Y - 1, NC // lay.batch)), dma((Y - 1, NC // lay.batch)),
             dma((CTX - 1,)), dma((CTX - 1,)), dma((DP - 1,)), dma((DP - 1,)),
         ],
         compiler_params=pltpu.CompilerParams(
-            collective_id=0, has_side_effects=True, vmem_limit_bytes=60 * 2**20
+            collective_id=0, has_side_effects=True, vmem_limit_bytes=44 * 2**20
         ),
         name="mixer",
     )(query_act, key_act, value_act, out_grad, filter_taps,

time: 73.1 us -> 67.5 us (0.923)
  Pallas kernels: 67.6 us -> 54.6 us
  local copies, waits for them, and re-layouts: 0.65 us -> 9.32 us
  other arithmetic: 4.03 us -> 2.45 us
    pallas_call x1, Pallas kernels: 67.6 us -> 54.6 us  [shards(): pl.pallas_call(functools.partial(kernel, lay, scale), in_specs=[any_spec]...]
    unnamed x9 -> x17, local copies, waits for them, and re-layouts: 0.65 us -> 9.32 us
    convert_element_type x1, other arithmetic: 4.03 us -> 2.45 us  [shards(): value_grad = (back * key_act.astype(F32)).astype(BF16)]
where the time goes in v5:
time: 67.5 us; the launch traced here: 67.1 us
  Pallas kernels  54.6 us (81%)
  local copies, waits for them, and re-layouts  9.32 us (14%)
  other arithmetic  2.45 us (4%)
    pallas_call x1, Pallas kernels, shards(): pl.pallas_call(functools.partial(kernel, lay, scale), in_specs=[any_spec]...  54.6 us
    unnamed x17, local copies, waits for them, and re-layouts  9.32 us
    convert_element_type x1, other arithmetic, shards(): value_grad = (back * key_act.astype(F32)).astype(BF16)  2.45 us

profile of v5, /device:TPU:1, one launch (start us, length us, event | category | flops | bytes accessed | tf_op | source)
XLA Modules:
  0.0 67.1 jit_solution(14778290177616706279)
XLA Ops:
  0.6 0.0 copy-start
  0.6 1.2 %copy-done = bf16[128,4096]{1,0:T(8,128)(2,1)S(1)} copy-done((bf16[128,4096]{1,0:T(8,128)(2,1)S(1)}, bf16[128,4096]{1,0:T(8,128)(2,1)}, u32[]{:S(2)}) %copy-start) | copy-done | bytes 1048600
  1.9 0.0 copy-start.1
  1.9 1.2 %copy-done.1 = bf16[128,4096]{1,0:T(8,128)(2,1)S(1)} copy-done((bf16[128,4096]{1,0:T(8,128)(2,1)S(1)}, bf16[128,4096]{1,0:T(8,128)(2,1)}, u32[]{:S(2)}) %copy-start.1) | copy-done | bytes 1048600
  3.1 0.0 copy-start.2
  3.1 1.2 %copy-done.2 = bf16[128,4096]{1,0:T(8,128)(2,1)S(1)} copy-done((bf16[128,4096]{1,0:T(8,128)(2,1)S(1)}, bf16[128,4096]{1,0:T(8,128)(2,1)}, u32[]{:S(2)}) %copy-start.2) | copy-done | bytes 1048600
  4.3 0.0 copy-start.3
  4.3 1.2 %copy-done.3 = bf16[128,4096]{1,0:T(8,128)(2,1)S(1)} copy-done((bf16[128,4096]{1,0:T(8,128)(2,1)S(1)}, bf16[128,4096]{1,0:T(8,128)(2,1)}, u32[]{:S(2)}) %copy-start.3) | copy-done | bytes 1048600
  5.5 0.0 copy-start.4
  5.5 1.1 %copy-done.4 = bf16[3,384,256]{2,1,0:T(8,128)(2,1)S(1)} copy-done((bf16[3,384,256]{2,1,0:T(8,128)(2,1)S(1)}, bf16[3,384,256]{2,1,0:T(8,128)(2,1)}, u32[]{:S(2)}) %copy-start.4) | copy-done | bytes 589848
  6.6 0.0 copy-start.5
  6.6 1.0 %copy-done.5 = bf16[2,256,384]{2,1,0:T(8,128)(2,1)S(1)} copy-done((bf16[2,256,384]{2,1,0:T(8,128)(2,1)S(1)}, bf16[2,256,384]{2,1,0:T(8,128)(2,1)}, u32[]{:S(2)}) %copy-start.5) | copy-done | bytes 393240
  7.6 0.0 copy-start.6
  7.6 0.9 %copy-done.6 = s32[32768]{0:T(1024)S(1)} copy-done((s32[32768]{0:T(1024)S(1)}, s32[32768]{0:T(1024)}, u32[]{:S(2)}) %copy-start.6) | copy-done | bytes 131096
  8.5 0.0 copy-start.7
  8.5 0.8 %copy-done.7 = f32[128,128]{1,0:T(8,128)S(1)} copy-done((f32[128,128]{1,0:T(8,128)S(1)}, f32[128,128]{1,0:T(8,128)}, u32[]{:S(2)}) %copy-start.7) | copy-done | bytes 65560
  9.3 54.6 %mixer.1 = (bf16[128,4096]{1,0:T(8,128)(2,1)S(1)}, bf16[128,4096]{1,0:T(8,128)(2,1)S(1)}, f32[128,128]{1,0:T(8,128)S(1)}) custom-call(bf16[128,4096]{1,0:T(8,128)(2,1)S(1)} %copy-done.3, bf16[128,4096]{1,0:T(8,128)(2,1)S(1)} %copy-done, bf16[128,4096]{1,0:T(8,128)(2,1)S(1)} %copy-done.1, bf16[128,4096]{1,0:T(8,128)(2,1)S(1)} %copy-done.2, ...), custom_call_target="tpu_custom_call" | custom-call | tf_op jit(solution)/shard_map/mixer/pallas_call | solution.py:374
  64.0 2.4 %fusion.1 = (bf16[128,4096]{1,0:T(8,128)(2,1)}, bf16[128,4096]{1,0:T(8,128)(2,1)}, bf16[128,4096]{1,0:T(8,128)(2,1)}) fusion(bf16[128,4096]{1,0:T(8,128)(2,1)S(1)} %get-tuple-element.8, bf16[128,4096]{1,0:T(8,128)(2,1)S(1)} %copy-done, bf16[128,4096]{1,0:T(8,128)(2,1)S(1)} %copy-done.1, bf16[128,4096]{1,0:T(8,128)(2,1)S(1)} %get-tuple-element.7, ...), kind=kLoop, calls=%fused_computation.3 | loop fusion | flops 5767168 | bytes 8388608 | tf_op jit(solution)/shard_map/convert_element_type | solution.py:406
  66.4 0.6 copy.13
Async XLA Ops:
  0.6 1.2 %copy-start = (bf16[128,4096]{1,0:T(8,128)(2,1)S(1)}, bf16[128,4096]{1,0:T(8,128)(2,1)}, u32[]{:S(2)}) copy-start(bf16[128,4096]{1,0:T(8,128)(2,1)} %k_hbm.1) | copy-start | bytes 3145732
  1.9 1.2 %copy-start.1 = (bf16[128,4096]{1,0:T(8,128)(2,1)S(1)}, bf16[128,4096]{1,0:T(8,128)(2,1)}, u32[]{:S(2)}) copy-start(bf16[128,4096]{1,0:T(8,128)(2,1)} %v_hbm.1) | copy-start | bytes 3145732
  3.1 1.2 %copy-start.2 = (bf16[128,4096]{1,0:T(8,128)(2,1)S(1)}, bf16[128,4096]{1,0:T(8,128)(2,1)}, u32[]{:S(2)}) copy-start(bf16[128,4096]{1,0:T(8,128)(2,1)} %o_hbm.1) | copy-start | bytes 3145732
  4.3 1.2 %copy-start.3 = (bf16[128,4096]{1,0:T(8,128)(2,1)S(1)}, bf16[128,4096]{1,0:T(8,128)(2,1)}, u32[]{:S(2)}) copy-start(bf16[128,4096]{1,0:T(8,128)(2,1)} %q_hbm.1) | copy-start | bytes 3145732
  5.5 1.1 %copy-start.4 = (bf16[3,384,256]{2,1,0:T(8,128)(2,1)S(1)}, bf16[3,384,256]{2,1,0:T(8,128)(2,1)}, u32[]{:S(2)}) copy-start(bf16[3,384,256]{2,1,0:T(8,128)(2,1)} %constant.4.clone.fwd_tab) | copy-start | bytes 1769476
  6.6 1.0 %copy-start.5 = (bf16[2,256,384]{2,1,0:T(8,128)(2,1)S(1)}, bf16[2,256,384]{2,1,0:T(8,128)(2,1)}, u32[]{:S(2)}) copy-start(bf16[2,256,384]{2,1,0:T(8,128)(2,1)} %constant.5.clone.inv_tab) | copy-start | bytes 1179652
  7.6 0.9 %copy-start.6 = (s32[32768]{0:T(1024)S(1)}, s32[32768]{0:T(1024)}, u32[]{:S(2)}) copy-start(s32[32768]{0:T(1024)} %param.13) | copy-start | bytes 393220
  8.5 0.8 %copy-start.7 = (f32[128,128]{1,0:T(8,128)S(1)}, f32[128,128]{1,0:T(8,128)}, u32[]{:S(2)}) copy-start(f32[128,128]{1,0:T(8,128)} %taps.1) | copy-start | bytes 196612

commit v6 on v5

--- a/solution.py
+++ b/solution.py
@@ -74,12 +74,12 @@
     )
 
 
-def kernel(lay, scale, q_hbm, k_hbm, v_hbm, o_hbm, taps, docs, fwd_tab, inv_tab,
+def kernel(lay, scale, q_hbm, k_hbm, v_hbm, o_hbm, taps_hbm, docs_hbm, fwd_hbm, inv_hbm,
            mixed_ref, back_ref, fg_ref,
-           q, k, v, o, p, g, p_prev, g_next, mixed, back, pa_hat, ga_hat, pb_hat, gb_hat,
+           taps, docs, fwd_tab, inv_tab, q, k, v, o, p, g, p_prev, g_next, mixed, back, pa_hat, ga_hat, pb_hat, gb_hat,
            e_own, e_prev, e_next, d_own, tap_own, tap_all, fg_part, c_recv, y_send, y_recv,
            x_own, x_send, x_recv, final,
-           in_sem, out_sem, p_ssem, p_rsem, g_ssem, g_rsem, tx_ssem, tx_rsem,
+           small_sem, in_sem, out_sem, p_ssem, p_rsem, g_ssem, g_rsem, tx_ssem, tx_rsem,
            ty_ssem, ty_rsem, tc_ssem, tc_rsem, c_ssem, c_rsem, y_ssem, y_rsem,
            x_ssem, x_rsem, f_ssem, f_rsem):
     dp, ctx = lax.axis_index("dp"), lax.axis_index("ctx")
@@ -119,12 +119,94 @@
             load(which, n).start()
         return carry
 
+    small = [
+        pltpu.make_async_copy(hbm, ref, small_sem.at[i])
+        for i, (hbm, ref) in enumerate(
+            ((taps_hbm, taps), (docs_hbm, docs), (fwd_hbm, fwd_tab), (inv_hbm, inv_tab))
+        )
+    ]
+    small[0].start()
     lax.fori_loop(0, HALF, start_loads, 0)
+    for copy in small[1:]:
+        copy.start()
+    small[0].wait()
 
     turned = taps[...].T.astype(BF16)
     tap_own[...] = turned.reshape(DP, lay.rows, lay.lanes)
     tap_all[slot, ctx] = tap_own[slot]
 
+    def tap_ctx(r):
+        here = tap_all.at[slot, ctx]
+        return remote(here, here, tx_ssem.at[r - 1], tx_rsem.at[r - 1], c_peer(r))
+
+    def tap_y(r):
+        here = tap_all.at[slot]
+        return remote(here, here, ty_ssem.at[r - 1], ty_rsem.at[r - 1], y_peer(r))
+
+    def tap_c():
+        here = tap_all.at[pl.ds(core * Y, Y)]
+        return remote(here, here, tc_ssem, tc_rsem, partner)
+
+    def halo_p(n):
+        return remote(p.at[n], p_prev.at[n], p_ssem.at[n], p_rsem.at[n], nxt)
+
+    def halo_g(n):
+        return remote(g.at[n], g_next.at[n], g_ssem.at[n], g_rsem.at[n], prv)
+
+    def pair(n):
+        return remote(fg_part.at[n, 1 - core], c_recv.at[n], c_ssem.at[n], c_rsem.at[n], partner)
+
+    def part_y(r, group):
+        chunks = pl.ds(group * YB, YB)
+        return remote(y_send.at[lax.rem(y + r, Y), chunks], y_recv.at[r - 1, chunks],
+                      y_ssem.at[r - 1, group], y_rsem.at[r - 1, group], y_peer(r))
+
+    def part_ctx(r):
+        return remote(x_send.at[lax.rem(ctx + r, CTX)], x_recv.at[r - 1],
+                      x_ssem.at[r - 1], x_rsem.at[r - 1], c_peer(r))
+
+    def each_peer(action):
+        def body(r, carry):
+            action(r)
+            return carry
+
+        lax.fori_loop(1, CTX, body, 0)
+
+    def part_f(r):
+        here = final.at[slot]
+        return remote(here, here, f_ssem.at[r - 1], f_rsem.at[r - 1], d_peer(r))
+
+    def produce(j):
+        for n in (j, j + HALF):
+            load(1, n).wait()
+            load(2, n).wait()
+            p[n] = (k[n].astype(F32) * v[n].astype(F32)).astype(BF16)
+            load(0, n).wait()
+            load(3, n).wait()
+            g[n] = (q[n].astype(F32) * o[n].astype(F32)).astype(BF16)
+
+    def send(n):
+        halo_p(n).start()
+        halo_g(lax.rem(n + HALF, NC)).start()
+
+    def produce_and_send(j, carry):
+        produce(j)
+        send(j)
+        return carry
+
+    def send_rest(n, carry):
+        send(n)
+        return carry
+
+    produce(0)
+    pl.semaphore_wait(barrier, len(peers) + CTX - 1)
+    each_peer(lambda r: tap_ctx(r).start())
+    send(0)
+    lax.fori_loop(1, HALF, produce_and_send, 0)
+    lax.fori_loop(HALF, NC, send_rest, 0)
+
+    for copy in small[1:]:
+        copy.wait()
     above, below = jnp.maximum(me - 1, 0), jnp.minimum(me + 1, DP * CTX - 1)
     own = docs[pl.ds(me, 1), :]
     first, last = own[:, :1], own[:, FL - 1 :]
@@ -145,76 +227,6 @@
         d0, d1 = inv_tab[0, rows, :].astype(F32), inv_tab[1, rows, :].astype(F32)
         d_own[rows, :] = (d0 * (1.0 - wide) + d1 * wide).astype(BF16)
 
-    def tap_ctx(r):
-        here = tap_all.at[slot, ctx]
-        return remote(here, here, tx_ssem.at[r - 1], tx_rsem.at[r - 1], c_peer(r))
-
-    def tap_y(r):
-        here = tap_all.at[slot]
-        return remote(here, here, ty_ssem.at[r - 1], ty_rsem.at[r - 1], y_peer(r))
-
-    def tap_c():
-        here = tap_all.at[pl.ds(core * Y, Y)]
-        return remote(here, here, tc_ssem, tc_rsem, partner)
-
-    def halo_p(n):
-        return remote(p.at[n], p_prev.at[n], p_ssem.at[n], p_rsem.at[n], nxt)
-
-    def halo_g(n):
-        return remote(g.at[n], g_next.at[n], g_ssem.at[n], g_rsem.at[n], prv)
-
-    def pair(n):
-        return remote(fg_part.at[n, 1 - core], c_recv.at[n], c_ssem.at[n], c_rsem.at[n], partner)
-
-    def part_y(r, group):
-        chunks = pl.ds(group * YB, YB)
-        return remote(y_send.at[lax.rem(y + r, Y), chunks], y_recv.at[r - 1, chunks],
-                      y_ssem.at[r - 1, group], y_rsem.at[r - 1, group], y_peer(r))
-
-    def part_ctx(r):
-        return remote(x_send.at[lax.rem(ctx + r, CTX)], x_recv.at[r - 1],
-                      x_ssem.at[r - 1], x_rsem.at[r - 1], c_peer(r))
-
-    def each_peer(action):
-        def body(r, carry):
-            action(r)
-            return carry
-
-        lax.fori_loop(1, CTX, body, 0)
-
-    def part_f(r):
-        here = final.at[slot]
-        return remote(here, here, f_ssem.at[r - 1], f_rsem.at[r - 1], d_peer(r))
-
-    def produce(j):
-        for n in (j, j + HALF):
-            load(1, n).wait()
-            load(2, n).wait()
-            p[n] = (k[n].astype(F32) * v[n].astype(F32)).astype(BF16)
-            load(0, n).wait()
-            load(3, n).wait()
-            g[n] = (q[n].astype(F32) * o[n].astype(F32)).astype(BF16)
-
-    def send(n):
-        halo_p(n).start()
-        halo_g(lax.rem(n + HALF, NC)).start()
-
-    def produce_and_send(j, carry):
-        produce(j)
-        send(j)
-        return carry
-
-    def send_rest(n, carry):
-        send(n)
-        return carry
-
-    produce(0)
-    pl.semaphore_wait(barrier, len(peers) + CTX - 1)
-    each_peer(lambda r: tap_ctx(r).start())
-    send(0)
-    lax.fori_loop(1, HALF, produce_and_send, 0)
-    lax.fori_loop(HALF, NC, send_rest, 0)
-
     def absorb(n):
         pair(n).wait_recv()
         y_send[:, n] = (fg_part[n, core] + c_recv[n]).astype(BF16)
@@ -373,10 +385,15 @@
     dma = pltpu.SemaphoreType.DMA
     mixed, back, filter_grad = pl.pallas_call(
         functools.partial(kernel, lay, scale),
-        in_specs=[any_spec] * 4 + [vmem] * 4,
+        in_specs=[pl.BlockSpec(memory_space=pltpu.HBM)] * 8,
         out_specs=[any_spec, any_spec, vmem],
         out_shape=[acts, acts, jax.ShapeDtypeStruct(filter_taps.shape, F32)],
-        scratch_shapes=[block] * 10 + [spectra] * 4 + [
+        scratch_shapes=[
+            pltpu.VMEM(filter_taps.shape, F32),
+            pltpu.VMEM((DP * CTX, FL), jnp.int32),
+            pltpu.VMEM(fwd_tab.shape, BF16),
+            pltpu.VMEM(inv_tab.shape, BF16),
+        ] + [block] * 10 + [spectra] * 4 + [
             mat, mat, mat,
             pltpu.VMEM((2 * FL, N), BF16),
             pltpu.VMEM((DP, lay.rows, lay.lanes), BF16),
@@ -389,7 +406,7 @@
             pltpu.VMEM((CTX, lay.rows, lay.lanes), BF16),
             pltpu.VMEM((CTX - 1, lay.rows, lay.lanes), BF16),
             pltpu.VMEM((DP, lay.rows, lay.lanes), F32),
-            dma((4, NC)), dma((2, NC)), dma((NC,)), dma((NC,)), dma((NC,)), dma((NC,)),
+            dma((4,)), dma((4, NC)), dma((2, NC)), dma((NC,)), dma((NC,)), dma((NC,)), dma((NC,)),
             dma((CTX - 1,)), dma((CTX - 1,)), dma((Y - 1,)), dma((Y - 1,)), dma, dma,
             dma((NC,)), dma((NC,)), dma((Y - 1, NC // lay.batch)), dma((Y - 1, NC // lay.batch)),
             dma((CTX - 1,)), dma((CTX - 1,)), dma((DP - 1,)), dma((DP - 1,)),
@@ -398,8 +415,11 @@
             collective_id=0, has_side_effects=True, vmem_limit_bytes=44 * 2**20
         ),
         name="mixer",
-    )(query_act, key_act, value_act, out_grad, filter_taps,
-      doc_ids.reshape(-1, FL), jnp.asarray(fwd_tab), jnp.asarray(inv_tab))
+    )(*(
+        pltpu.with_memory_space_constraint(array, pltpu.HBM)
+        for array in (query_act, key_act, value_act, out_grad, filter_taps,
+                      doc_ids.reshape(-1, FL), jnp.asarray(fwd_tab), jnp.asarray(inv_tab))
+    ))
     mixed, back = mixed.astype(F32), back.astype(F32)
     query_grad = (out_grad.astype(F32) * mixed).astype(BF16)
     key_grad = (back * value_act.astype(F32)).astype(BF16)

time: 67.5 us -> 58.9 us (0.87)
  local copies, waits for them, and re-layouts: 9.32 us -> 0.64 us
    unnamed x17 -> x7, local copies, waits for them, and re-layouts: 9.32 us -> 0.64 us
where the time goes in v6:
time: 58.9 us; the launch traced here: 58.8 us
  Pallas kernels  55 us (93%)
  other arithmetic  2.45 us (4%)
  between operations  0.69 us (1%)
  local copies, waits for them, and re-layouts  0.64 us (1%)
    pallas_call x1, Pallas kernels, shards(): pl.pallas_call(functools.partial(kernel, lay, scale), in_specs=[pl.BlockS...  55 us
    convert_element_type x1, other arithmetic, shards(): value_grad = (back * key_act.astype(F32)).astype(BF16)  2.45 us

profile of v6, /device:TPU:1, one launch (start us, length us, event | category | flops | bytes accessed | tf_op | source)
XLA Modules:
  0.0 58.8 jit_solution(15173907673626388164)
XLA Ops:
  0.6 0.0 copy-start
  0.6 0.0 copy-start.1
  0.7 0.0 copy-start.2
  0.7 55.0 %mixer.1 = (bf16[128,4096]{1,0:T(8,128)(2,1)S(1)}, bf16[128,4096]{1,0:T(8,128)(2,1)S(1)}, f32[128,128]{1,0:T(8,128)S(1)}) custom-call(bf16[128,4096]{1,0:T(8,128)(2,1)} %q_hbm.1, bf16[128,4096]{1,0:T(8,128)(2,1)} %k_hbm.1, bf16[128,4096]{1,0:T(8,128)(2,1)} %v_hbm.1, bf16[128,4096]{1,0:T(8,128)(2,1)} %o_hbm.1, f32[128,128]{1,0:T(8,128)} %taps_hbm.1, ...), custom_call_target="tpu_custom_call" | custom-call | tf_op jit(solution)/shard_map/mixer/pallas_call | solution.py:386
  55.7 0.0 copy-done
  55.7 0.0 copy-done.1
  55.7 0.0 copy-done.2
  55.7 2.4 %fusion.1 = (bf16[128,4096]{1,0:T(8,128)(2,1)}, bf16[128,4096]{1,0:T(8,128)(2,1)}, bf16[128,4096]{1,0:T(8,128)(2,1)}) fusion(bf16[128,4096]{1,0:T(8,128)(2,1)S(1)} %get-tuple-element.8, bf16[128,4096]{1,0:T(8,128)(2,1)S(1)} %copy-done, bf16[128,4096]{1,0:T(8,128)(2,1)S(1)} %copy-done.1, bf16[128,4096]{1,0:T(8,128)(2,1)S(1)} %get-tuple-element.7, ...), kind=kLoop, calls=%fused_computation.3 | loop fusion | flops 5767168 | bytes 8388608 | tf_op jit(solution)/shard_map/convert_element_type | solution.py:426
  58.2 0.6 %copy.13 = f32[128,128]{1,0:T(8,128)} copy(f32[128,128]{1,0:T(8,128)S(1)} %get-tuple-element.20) | data formatting | bytes 131072
Async XLA Ops:
  0.6 55.0 %copy-start = (bf16[128,4096]{1,0:T(8,128)(2,1)S(1)}, bf16[128,4096]{1,0:T(8,128)(2,1)}, u32[]{:S(2)}) copy-start(bf16[128,4096]{1,0:T(8,128)(2,1)} %k_hbm.1) | copy-start | bytes 3145732
  0.6 55.0 %copy-start.1 = (bf16[128,4096]{1,0:T(8,128)(2,1)S(1)}, bf16[128,4096]{1,0:T(8,128)(2,1)}, u32[]{:S(2)}) copy-start(bf16[128,4096]{1,0:T(8,128)(2,1)} %v_hbm.1) | copy-start | bytes 3145732
  0.7 55.0 %copy-start.2 = (bf16[128,4096]{1,0:T(8,128)(2,1)S(1)}, bf16[128,4096]{1,0:T(8,128)(2,1)}, u32[]{:S(2)}) copy-start(bf16[128,4096]{1,0:T(8,128)(2,1)} %o_hbm.1) | copy-start | bytes 3145732

commit v7 on v6

--- a/solution.py
+++ b/solution.py
@@ -63,6 +63,8 @@
         self.chunks = chans // chunk
         self.half = self.chunks // 2
         self.batch = max(1, self.half // 4)
+        self.sum_step = min(4, self.half - 1)
+        self.held = min(3, self.half - self.sum_step)
         self.rows = FL // dp
         self.lanes = chans // ctx
 
@@ -203,7 +205,7 @@
     each_peer(lambda r: tap_ctx(r).start())
     send(0)
     lax.fori_loop(1, HALF, produce_and_send, 0)
-    lax.fori_loop(HALF, NC, send_rest, 0)
+    lax.fori_loop(HALF, NC - lay.held, send_rest, 0)
 
     for copy in small[1:]:
         copy.wait()
@@ -260,6 +262,7 @@
             x_own[i] = piece
             x_send[i] = piece.astype(BF16)
         each_peer(lambda r: part_ctx(r).start())
+        lax.fori_loop(NC - lay.held, NC, send_rest, 0)
 
     def sum_ctx():
         each_peer(lambda r: part_ctx(r).wait_recv())
@@ -273,7 +276,7 @@
                 pl.when(j == step)(event)
 
     early = ((0, relay_y), (min(5, HALF - 1), relay_c))
-    late = ((4, sum_y), (HALF, sum_ctx))
+    late = ((lay.sum_step, sum_y), (HALF - 2 if HALF >= 8 else HALF, sum_ctx))
 
     def first_half(j, carry):
         scheduled(j, early)

time: 58.9 us -> 61 us (1.036)
  Pallas kernels: 55 us -> 57.2 us
    pallas_call x1, Pallas kernels: 55 us -> 57.2 us  [shards(): pl.pallas_call(functools.partial(kernel, lay, scale), in_specs=[pl.BlockS...]
where the time goes in v7:
time: 61 us
  Pallas kernels  57.2 us (94%)
  other arithmetic  2.45 us (4%)
  between operations  0.69 us (1%)
  local copies, waits for them, and re-layouts  0.64 us (1%)
    pallas_call x1, Pallas kernels, shards(): pl.pallas_call(functools.partial(kernel, lay, scale), in_specs=[pl.BlockS...  57.2 us
    convert_element_type x1, other arithmetic, shards(): value_grad = (back * key_act.astype(F32)).astype(BF16)  2.45 us

profile of v7, /device:TPU:1, one launch (start us, length us, event | category | flops | bytes accessed | tf_op | source)
XLA Modules:
  0.0 61.0 jit_solution(10243835739405764609)
XLA Ops:
  0.6 0.0 copy-start
  0.6 0.0 copy-start.1
  0.7 0.0 copy-start.2
  0.7 57.2 %mixer.1 = (bf16[128,4096]{1,0:T(8,128)(2,1)S(1)}, bf16[128,4096]{1,0:T(8,128)(2,1)S(1)}, f32[128,128]{1,0:T(8,128)S(1)}) custom-call(bf16[128,4096]{1,0:T(8,128)(2,1)} %q_hbm.1, bf16[128,4096]{1,0:T(8,128)(2,1)} %k_hbm.1, bf16[128,4096]{1,0:T(8,128)(2,1)} %v_hbm.1, bf16[128,4096]{1,0:T(8,128)(2,1)} %o_hbm.1, f32[128,128]{1,0:T(8,128)} %taps_hbm.1, ...), custom_call_target="tpu_custom_call" | custom-call | tf_op jit(solution)/shard_map/mixer/pallas_call | solution.py:389
  57.9 0.0 copy-done
  57.9 0.0 copy-done.1
  57.9 0.0 copy-done.2
  57.9 2.4 %fusion.1 = (bf16[128,4096]{1,0:T(8,128)(2,1)}, bf16[128,4096]{1,0:T(8,128)(2,1)}, bf16[128,4096]{1,0:T(8,128)(2,1)}) fusion(bf16[128,4096]{1,0:T(8,128)(2,1)S(1)} %get-tuple-element.8, bf16[128,4096]{1,0:T(8,128)(2,1)S(1)} %copy-done, bf16[128,4096]{1,0:T(8,128)(2,1)S(1)} %copy-done.1, bf16[128,4096]{1,0:T(8,128)(2,1)S(1)} %get-tuple-element.7, ...), kind=kLoop, calls=%fused_computation.3 | loop fusion | flops 5767168 | bytes 8388608 | tf_op jit(solution)/shard_map/convert_element_type | solution.py:429
  60.3 0.6 %copy.13 = f32[128,128]{1,0:T(8,128)} copy(f32[128,128]{1,0:T(8,128)S(1)} %get-tuple-element.20) | data formatting | bytes 131072
Async XLA Ops:
  0.6 57.2 %copy-start = (bf16[128,4096]{1,0:T(8,128)(2,1)S(1)}, bf16[128,4096]{1,0:T(8,128)(2,1)}, u32[]{:S(2)}) copy-start(bf16[128,4096]{1,0:T(8,128)(2,1)} %k_hbm.1) | copy-start | bytes 3145732
  0.6 57.2 %copy-start.1 = (bf16[128,4096]{1,0:T(8,128)(2,1)S(1)}, bf16[128,4096]{1,0:T(8,128)(2,1)}, u32[]{:S(2)}) copy-start(bf16[128,4096]{1,0:T(8,128)(2,1)} %v_hbm.1) | copy-start | bytes 3145732
  0.7 57.2 %copy-start.2 = (bf16[128,4096]{1,0:T(8,128)(2,1)S(1)}, bf16[128,4096]{1,0:T(8,128)(2,1)}, u32[]{:S(2)}) copy-start(bf16[128,4096]{1,0:T(8,128)(2,1)} %o_hbm.1) | copy-start | bytes 3145732

commit v8 on v6

--- a/solution.py
+++ b/solution.py
@@ -63,6 +63,7 @@
         self.chunks = chans // chunk
         self.half = self.chunks // 2
         self.batch = max(1, self.half // 4)
+        self.sum_step = min(6, self.half - 1)
         self.rows = FL // dp
         self.lanes = chans // ctx
 
@@ -75,8 +76,8 @@
 
 
 def kernel(lay, scale, q_hbm, k_hbm, v_hbm, o_hbm, taps_hbm, docs_hbm, fwd_hbm, inv_hbm,
-           mixed_ref, back_ref, fg_ref,
-           taps, docs, fwd_tab, inv_tab, q, k, v, o, p, g, p_prev, g_next, mixed, back, pa_hat, ga_hat, pb_hat, gb_hat,
+           qg_ref, kg_ref, vg_ref, fg_ref,
+           taps, docs, fwd_tab, inv_tab, q, k, v, o, p, g, p_prev, g_next, qg, kg, vg, pa_hat, ga_hat, pb_hat, gb_hat,
            e_own, e_prev, e_next, d_own, tap_own, tap_all, fg_part, c_recv, y_send, y_recv,
            x_own, x_send, x_recv, final,
            small_sem, in_sem, out_sem, p_ssem, p_rsem, g_ssem, g_rsem, tx_ssem, tx_rsem,
@@ -272,8 +273,8 @@
             if step < HALF:
                 pl.when(j == step)(event)
 
-    early = ((0, relay_y), (min(5, HALF - 1), relay_c))
-    late = ((4, sum_y), (HALF, sum_ctx))
+    early = ((0, relay_y), (min(7, HALF - 1), relay_c))
+    late = ((lay.sum_step, sum_y), (HALF, sum_ctx))
 
     def first_half(j, carry):
         scheduled(j, early)
@@ -316,13 +317,21 @@
             [tap_all[:, n * per + i].reshape(FL, lay.lanes) for i in range(per)], 1
         )
 
-    def write(ref, n, value):
-        ref[n] = (value * (1.0 / BINS)).astype(BF16)
+    def rounded(value):
+        return (value * (1.0 / BINS)).astype(BF16).astype(F32)
+
+    def write_query(n, value):
+        qg[n] = (o[n].astype(F32) * rounded(value)).astype(BF16)
+
+    def write_kv(n, value):
+        back = rounded(value)
+        kg[n] = (back * v[n].astype(F32)).astype(BF16)
+        vg[n] = (back * k[n].astype(F32)).astype(BF16)
 
     def store(which, n):
-        ref, hbm = ((mixed, mixed_ref), (back, back_ref))[which]
+        ref, out = ((qg, qg_ref), (kg, kg_ref), (vg, vg_ref))[which]
         return pltpu.make_async_copy(
-            ref.at[n], hbm.at[:, pl.ds(pl.multiple_of(n * CH, CH), CH)], out_sem.at[which, n]
+            ref.at[n], out.at[:, pl.ds(pl.multiple_of(n * CH, CH), CH)], out_sem.at[which, n]
         )
 
     def second_half(j, carry):
@@ -334,13 +343,13 @@
         hb = forward(fwd_tab[0], taps_of(b))
         ga = ga_hat[j] + forward(e_next[...], g_next[a])
         pb = pb_hat[j] + forward(e_prev[...], p_prev[b])
-        write(mixed, a, inverse(d_own[...], *convolve(ha, pa_hat[j])))
-        write(back, a, inverse(d_own[...], *correlate(ha, ga)))
-        write(mixed, b, inverse(d_own[...], *convolve(hb, pb)))
-        write(back, b, inverse(d_own[...], *correlate(hb, gb_hat[j])))
+        write_query(a, inverse(d_own[...], *convolve(ha, pa_hat[j])))
+        write_kv(a, inverse(d_own[...], *correlate(ha, ga)))
+        write_query(b, inverse(d_own[...], *convolve(hb, pb)))
+        write_kv(b, inverse(d_own[...], *correlate(hb, gb_hat[j])))
         for n in (a, b):
-            store(0, n).start()
-            store(1, n).start()
+            for which in range(3):
+                store(which, n).start()
         return carry
 
     lax.fori_loop(0, HALF, second_half, 0)
@@ -355,8 +364,8 @@
         halo_p(n).wait_send()
         halo_g(n).wait_send()
         pair(n).wait_send()
-        store(0, n).wait()
-        store(1, n).wait()
+        for which in range(3):
+            store(which, n).wait()
         return carry
 
     lax.fori_loop(0, NC, drain, 0)
@@ -369,6 +378,22 @@
     for r in range(1, DP):
         part_f(r).wait_send()
     tap_c().wait_send()
+
+
+def put_out(*refs):
+    sem = refs[8]
+    copies = []
+    for i in range(4):
+        half = refs[i].shape[0] // 2
+        for j in range(2):
+            rows = pl.ds(j * half, half)
+            copies.append(
+                pltpu.make_async_copy(refs[i].at[rows], refs[4 + i].at[rows], sem.at[i, j])
+            )
+    for copy in copies:
+        copy.start()
+    for copy in copies:
+        copy.wait()
 
 
 def shards(query_act, key_act, value_act, out_grad, filter_taps, doc_ids):
@@ -383,17 +408,17 @@
     spectra = pltpu.VMEM((lay.half, N, CH), F32)
     mat = pltpu.VMEM((N, 2 * FL), BF16)
     dma = pltpu.SemaphoreType.DMA
-    mixed, back, filter_grad = pl.pallas_call(
+    results = pl.pallas_call(
         functools.partial(kernel, lay, scale),
         in_specs=[pl.BlockSpec(memory_space=pltpu.HBM)] * 8,
-        out_specs=[any_spec, any_spec, vmem],
-        out_shape=[acts, acts, jax.ShapeDtypeStruct(filter_taps.shape, F32)],
+        out_specs=[any_spec] * 3 + [vmem],
+        out_shape=[acts, acts, acts, jax.ShapeDtypeStruct(filter_taps.shape, F32)],
         scratch_shapes=[
             pltpu.VMEM(filter_taps.shape, F32),
             pltpu.VMEM((DP * CTX, FL), jnp.int32),
             pltpu.VMEM(fwd_tab.shape, BF16),
             pltpu.VMEM(inv_tab.shape, BF16),
-        ] + [block] * 10 + [spectra] * 4 + [
+        ] + [block] * 11 + [spectra] * 4 + [
             mat, mat, mat,
             pltpu.VMEM((2 * FL, N), BF16),
             pltpu.VMEM((DP, lay.rows, lay.lanes), BF16),
@@ -406,7 +431,7 @@
             pltpu.VMEM((CTX, lay.rows, lay.lanes), BF16),
             pltpu.VMEM((CTX - 1, lay.rows, lay.lanes), BF16),
             pltpu.VMEM((DP, lay.rows, lay.lanes), F32),
-            dma((4,)), dma((4, NC)), dma((2, NC)), dma((NC,)), dma((NC,)), dma((NC,)), dma((NC,)),
+            dma((4,)), dma((4, NC)), dma((3, NC)), dma((NC,)), dma((NC,)), dma((NC,)), dma((NC,)),
             dma((CTX - 1,)), dma((CTX - 1,)), dma((Y - 1,)), dma((Y - 1,)), dma, dma,
             dma((NC,)), dma((NC,)), dma((Y - 1, NC // lay.batch)), dma((Y - 1, NC // lay.batch)),
             dma((CTX - 1,)), dma((CTX - 1,)), dma((DP - 1,)), dma((DP - 1,)),
@@ -420,11 +445,15 @@
         for array in (query_act, key_act, value_act, out_grad, filter_taps,
                       doc_ids.reshape(-1, FL), jnp.asarray(fwd_tab), jnp.asarray(inv_tab))
     ))
-    mixed, back = mixed.astype(F32), back.astype(F32)
-    query_grad = (out_grad.astype(F32) * mixed).astype(BF16)
-    key_grad = (back * value_act.astype(F32)).astype(BF16)
-    value_grad = (back * key_act.astype(F32)).astype(BF16)
-    return query_grad, key_grad, value_grad, filter_grad
+    return pl.pallas_call(
+        put_out,
+        in_specs=[any_spec] * 4,
+        out_specs=[any_spec] * 4,
+        out_shape=[acts, acts, acts, jax.ShapeDtypeStruct(filter_taps.shape, F32)],
+        scratch_shapes=[dma((4, 2))],
+        compiler_params=pltpu.CompilerParams(vmem_limit_bytes=8 * 2**20),
+        name="put_out",
+    )(*results)
 
 
 def solution(mesh):

time: 58.9 us -> 57.6 us (0.978)
  other arithmetic: 2.45 us -> 0 us
  Pallas kernels: 55 us -> 56.9 us
  local copies, waits for them, and re-layouts: 0.64 us -> 0 us
    convert_element_type x1 -> x0, other arithmetic: 2.45 us -> none  [shards(): value_grad = (back * key_act.astype(F32)).astype(BF16)]
    pallas_call x0 -> x1, Pallas kernels: none -> 1.73 us  [shards(): pl.pallas_call(put_out, in_specs=[any_spec] * 4, out_specs=[any_spec] * 4...]
    unnamed x7 -> x0, local copies, waits for them, and re-layouts: 0.64 us -> none
where the time goes in v8:
time: 57.6 us; the launch traced here: 57.5 us
  Pallas kernels  56.9 us (99%)
  between operations  0.64 us (1%)
    pallas_call x1, Pallas kernels, shards(): pl.pallas_call(functools.partial(kernel, lay, scale), in_specs=[pl.BlockS...  55.1 us
    pallas_call x1, Pallas kernels, shards(): pl.pallas_call(put_out, in_specs=[any_spec] * 4, out_specs=[any_spec] * 4...  1.73 us

profile of v8, /device:TPU:1, one launch (start us, length us, event | category | flops | bytes accessed | tf_op | source)
XLA Modules:
  0.0 57.5 jit_solution(9083509180508926986)
XLA Ops:
  0.6 55.1 %mixer.1 = (bf16[128,4096]{1,0:T(8,128)(2,1)S(1)}, bf16[128,4096]{1,0:T(8,128)(2,1)S(1)}, bf16[128,4096]{1,0:T(8,128)(2,1)S(1)}, f32[128,128]{1,0:T(8,128)S(1)}) custom-call(bf16[128,4096]{1,0:T(8,128)(2,1)} %q_hbm.1, bf16[128,4096]{1,0:T(8,128)(2,1)} %k_hbm.1, bf16[128,4096]{1,0:T(8,128)(2,1)} %v_hbm.1, bf16[128,4096]{1,0:T(8,128)(2,1)} %o_hbm.1, ...), custom_call_target="tpu_custom_call" | custom-call | tf_op jit(solution)/shard_map/mixer/pallas_call | solution.py:411
  55.8 1.7 %put_out.1 = (bf16[128,4096]{1,0:T(8,128)(2,1)}, bf16[128,4096]{1,0:T(8,128)(2,1)}, bf16[128,4096]{1,0:T(8,128)(2,1)}, f32[128,128]{1,0:T(8,128)}) custom-call(bf16[128,4096]{1,0:T(8,128)(2,1)S(1)} %get-tuple-element.8.refs_0_, bf16[128,4096]{1,0:T(8,128)(2,1)S(1)} %get-tuple-element.9.refs_1_, bf16[128,4096]{1,0:T(8,128)(2,1)S(1)} %get-tuple-element.10.refs_2_, ...), custom_call_target="tpu_custom_call" | custom-call | tf_op jit(solution)/shard_map/put_out/pallas_call | solution.py:448

commit v9 on v8

--- a/solution.py
+++ b/solution.py
@@ -97,17 +97,6 @@
     partner = (2 * y + 1 - core, ctx)
     slot = core * Y + y
 
-    barrier = pltpu.get_barrier_semaphore()
-    peers = [nxt, prv] + [d_peer(r) for r in range(1, DP)]
-    for peer in peers:
-        pl.semaphore_signal(barrier, inc=1, device_id=peer, device_id_type=MESH)
-
-    def greet(r, carry):
-        pl.semaphore_signal(barrier, inc=1, device_id=c_peer(r), device_id_type=MESH)
-        return carry
-
-    lax.fori_loop(1, CTX, greet, 0)
-
     def load(which, n):
         hbm, ref = ((q_hbm, q), (k_hbm, k), (v_hbm, v), (o_hbm, o))[which]
         return pltpu.make_async_copy(
@@ -126,16 +115,22 @@
             ((taps_hbm, taps), (docs_hbm, docs), (fwd_hbm, fwd_tab), (inv_hbm, inv_tab))
         )
     ]
+    start_loads(0, 0)
     small[0].start()
-    lax.fori_loop(0, HALF, start_loads, 0)
+    barrier = pltpu.get_barrier_semaphore()
+    peers = [nxt, prv] + [d_peer(r) for r in range(1, DP)]
+    for peer in peers:
+        pl.semaphore_signal(barrier, inc=1, device_id=peer, device_id_type=MESH)
+
+    def greet(r, carry):
+        pl.semaphore_signal(barrier, inc=1, device_id=c_peer(r), device_id_type=MESH)
+        return carry
+
+    lax.fori_loop(1, CTX, greet, 0)
+
+    lax.fori_loop(1, HALF, start_loads, 0)
     for copy in small[1:]:
         copy.start()
-    small[0].wait()
-
-    turned = taps[...].T.astype(BF16)
-    tap_own[...] = turned.reshape(DP, lay.rows, lay.lanes)
-    tap_all[slot, ctx] = tap_own[slot]
-
     def tap_ctx(r):
         here = tap_all.at[slot, ctx]
         return remote(here, here, tx_ssem.at[r - 1], tx_rsem.at[r - 1], c_peer(r))
@@ -201,8 +196,13 @@
 
     produce(0)
     pl.semaphore_wait(barrier, len(peers) + CTX - 1)
+    send(0)
+    small[0].wait()
+
+    turned = taps[...].T.astype(BF16)
+    tap_own[...] = turned.reshape(DP, lay.rows, lay.lanes)
+    tap_all[slot, ctx] = tap_own[slot]
     each_peer(lambda r: tap_ctx(r).start())
-    send(0)
     lax.fori_loop(1, HALF, produce_and_send, 0)
     lax.fori_loop(HALF, NC, send_rest, 0)
 

time: 57.6 us -> 58.2 us (1.010)
  no operation moved by 1% of the time
where the time goes in v9:
time: 58.2 us; the launch traced here: 58.1 us
  Pallas kernels  57.4 us (99%)
  between operations  0.64 us (1%)
    pallas_call x1, Pallas kernels, shards(): pl.pallas_call(functools.partial(kernel, lay, scale), in_specs=[pl.BlockS...  55.7 us
    pallas_call x1, Pallas kernels, shards(): pl.pallas_call(put_out, in_specs=[any_spec] * 4, out_specs=[any_spec] * 4...  1.73 us

profile of v9, /device:TPU:1, one launch (start us, length us, event | category | flops | bytes accessed | tf_op | source)
XLA Modules:
  0.0 58.1 jit_solution(9410820988946676430)
XLA Ops:
  0.6 55.7 %mixer.1 = (bf16[128,4096]{1,0:T(8,128)(2,1)S(1)}, bf16[128,4096]{1,0:T(8,128)(2,1)S(1)}, bf16[128,4096]{1,0:T(8,128)(2,1)S(1)}, f32[128,128]{1,0:T(8,128)S(1)}) custom-call(bf16[128,4096]{1,0:T(8,128)(2,1)} %q_hbm.1, bf16[128,4096]{1,0:T(8,128)(2,1)} %k_hbm.1, bf16[128,4096]{1,0:T(8,128)(2,1)} %v_hbm.1, bf16[128,4096]{1,0:T(8,128)(2,1)} %o_hbm.1, ...), custom_call_target="tpu_custom_call" | custom-call | tf_op jit(solution)/shard_map/mixer/pallas_call | solution.py:411
  56.3 1.7 %put_out.1 = (bf16[128,4096]{1,0:T(8,128)(2,1)}, bf16[128,4096]{1,0:T(8,128)(2,1)}, bf16[128,4096]{1,0:T(8,128)(2,1)}, f32[128,128]{1,0:T(8,128)}) custom-call(bf16[128,4096]{1,0:T(8,128)(2,1)S(1)} %get-tuple-element.8.refs_0_, bf16[128,4096]{1,0:T(8,128)(2,1)S(1)} %get-tuple-element.9.refs_1_, bf16[128,4096]{1,0:T(8,128)(2,1)S(1)} %get-tuple-element.10.refs_2_, ...), custom_call_target="tpu_custom_call" | custom-call | tf_op jit(solution)/shard_map/put_out/pallas_call | solution.py:448
